TPU v7x, 32 devices: a whole 2x2x4 slice. The times are simulated.
32 devices in a mesh: row: 8 (over y, x, core), col: 4 (over z).
Axes of the slice: x: 2, y: 2, z: 4, core: 2. Of those that a mesh axis runs over, the one named last changes fastest.
Arguments:
- solution: float32 [64, 32768], P(None, ('row', 'col')), may hold values from -6 to 6
- residual: float32 [64, 65536], P(None, ('row', 'col')), may hold values from -6 to 6
- direction: float32 [64, 32768], P(None, ('row', 'col')), may hold values from -6 to 6
- jacobian_tiles: bfloat16 [512, 20, 128, 128], P('row', 'col'), may hold values from -0.125 to 0.125
- tile_blocks: int32 [512, 20], P('row', 'col'), may hold values from 0 to 63, as said below
- tile_counts: int32 [512, 4], P('row', 'col'), may hold values from 1 to 5, as said below
Outputs:
- solution_next: float32 [64, 32768], P(None, ('row', 'col'))
- residual_next: float32 [64, 65536], P(None, ('row', 'col'))
- direction_next: float32 [64, 32768], P(None, ('row', 'col'))
Inputs may be any that keep to these rules, and one draw needn't show every extreme that they name: `tile_blocks`: within each sensor and parameter group the 5 entries are different. Only the first tile_counts[i, c] slots of sensor i in group c hold a tile; some sensor fills all 5 slots of every group.
All inputs are finite; a program needn't handle non-finite values.
Results may differ from a plain program's by a relative error of at most 0.023.
Values may be sent and summed in bfloat16 or wider, within the bound.
No kernel may reach another device: no remote copies, remote signals or barrier semaphores. Data moves between devices by JAX's collectives and lax.ppermute only.
A program may use at most 128 MiB of HBM per device.

v0:
```python
import jax
import jax.numpy as jnp
from jax import lax
from jax.sharding import PartitionSpec as P

CB_DEV = 64
ITERS = 2


def times_highest(left, right):
    return jnp.dot(left, right, precision=lax.Precision.HIGHEST)


def gram_matrix(values):
    return jnp.dot(values, values.T, precision=lax.Precision.HIGHEST)


def solve_spd(matrix, right):
    factor_low = jnp.linalg.cholesky(matrix)
    middle = lax.linalg.triangular_solve(factor_low, right, left_side=True, lower=True)
    return lax.linalg.triangular_solve(
        factor_low, middle, left_side=True, lower=True, transpose_a=True
    )


def images(jacobian_tiles, tile_blocks, live_slot, direction_half):
    rhs_count = direction_half.shape[0]
    tile_width = jacobian_tiles.shape[2]
    table_view = direction_half.reshape(rhs_count, -1, tile_width)
    picked = jnp.take(table_view, tile_blocks, axis=1) * live_slot[None, :, :, None]
    product = jnp.einsum(
        "rsab,nrsb->nra", jacobian_tiles, picked, preferred_element_type=jnp.float32
    )
    return product.reshape(rhs_count, -1)


def gradients(jacobian_tiles, tile_blocks, live_slot, rows_half):
    rhs_count = rows_half.shape[0]
    tile_width = jacobian_tiles.shape[2]
    sensors = jacobian_tiles.shape[0]
    row_view = rows_half.reshape(rhs_count, sensors, tile_width)
    contrib = jnp.einsum(
        "rsab,nra->rsnb", jacobian_tiles, row_view, preferred_element_type=jnp.float32
    )
    contrib = contrib * live_slot.astype(jnp.float32)[:, :, None, None]
    summed = jax.ops.segment_sum(
        contrib.reshape(-1, rhs_count, tile_width), tile_blocks.reshape(-1), num_segments=CB_DEV
    )
    return summed.transpose(1, 0, 2).reshape(rhs_count, CB_DEV * tile_width)


def per_device(solution, residual, direction, jacobian_tiles, tile_blocks, tile_counts):
    live_slot = (
        jnp.arange(jacobian_tiles.shape[1], dtype=jnp.int32)[None, :] < tile_counts
    ).astype(jnp.bfloat16)
    share_rows = residual.shape[1]
    col_start = lax.axis_index("col") * share_rows
    rows_now = lax.all_gather(residual.astype(jnp.bfloat16), "col", axis=1, tiled=True).astype(
        residual.dtype
    )

    def gradient_step(rows_value):
        rows_half = rows_value.astype(jnp.bfloat16)
        partial_term = gradients(jacobian_tiles, tile_blocks, live_slot, rows_half)
        gradient = lax.psum_scatter(
            partial_term.astype(jnp.bfloat16), "row", scatter_dimension=1, tiled=True
        ).astype(jnp.float32)
        gamma_value = lax.psum(gram_matrix(gradient), ("row", "col"))
        return (gradient, gamma_value)

    gradient, gamma_now = gradient_step(rows_now)
    iterate = solution
    for iteration in range(ITERS):
        direction_half = lax.all_gather(direction.astype(jnp.bfloat16), "row", axis=1, tiled=True)
        image_partial_term = images(jacobian_tiles, tile_blocks, live_slot, direction_half)
        image = lax.psum(image_partial_term.astype(jnp.bfloat16), "col").astype(jnp.float32)
        curvature = lax.psum(gram_matrix(image), "row")
        image, curvature = (image, curvature)
        step_alpha = solve_spd(curvature, gamma_now)
        iterate = iterate + times_highest(step_alpha.T, direction)
        rows_now = rows_now - times_highest(step_alpha.T, image)
        gradient, gamma_next = gradient_step(rows_now)
        step_beta = solve_spd(gamma_now, gamma_next)
        direction = gradient + times_highest(step_beta.T, direction)
        gamma_now = gamma_next
    residual_out = lax.dynamic_slice_in_dim(rows_now, col_start, share_rows, 1)
    return (iterate, residual_out, direction)


def solution(mesh):
    placed = (
        P(None, ("row", "col")),
        P(None, ("row", "col")),
        P(None, ("row", "col")),
        P("row", "col", None, None),
        P("row", "col"),
        P("row", "col"),
    )
    return jax.shard_map(
        per_device,
        mesh=mesh,
        in_specs=placed,
        out_specs=(P(None, ("row", "col")), P(None, ("row", "col")), P(None, ("row", "col"))),
        check_vma=False,
    )
```

profile of v0, /device:TPU:0, one launch (start us, length us, event | category | flops | bytes accessed | tf_op | source)
XLA Modules:
  0.0 650.3 jit_solution(2488741487716216295)
XLA Ops:
  7.2 1.8 convert_element_type.98
  9.1 1.6 convert_element_type.93
  14.2 26.7 %all-gather.6.cloned.1.call-done = bf16[64,8192]{1,0:T(8,128)(2,1)} async-done(((bf16[64,2048]{1,0:T(8,128)(2,1)}), bf16[64,8192]{1,0:T(8,128)(2,1)}) %all-gather.6.cloned.1.call-update) | async-done | bytes 1048592 | tf_op jit(solution)/shard_map/all_gather | solution.py:58
  40.9 1.5 copy.89
  42.4 10.2 %broadcast_multiply_fusion.2 = f32[64,64,5,128]{3,1,2,0:T(8,128)} fusion(f32[64,5]{1,0:T(8,128)S(1)} %get-tuple-element.8, bf16[64,5,128,128]{3,2,1,0:T(8,128)(2,1)} %param.16, bf16[64,64,128,1]{2,1,0,3:T(8,128)(2,1)S(1)} %bitcast.184), kind=kOutput, calls=%fused_computation.15 | convolution fusion | flops 673710080 | bytes 22021376 | tf_op jit(solution)/shard_map/rsab,nra->rsnb/dot_general | solution.py:42
  52.8 33.0 %scatter_fusion = f32[64,64,128]{2,1,0:T(8,128)S(1)} fusion(f32[64,64,128]{2,1,0:T(8,128)S(1)} %broadcast.76.clone, s32[320]{0:T(512)S(1)} %reshape.148, f32[320,64,128]{2,1,0:T(8,128)} %bitcast.178), kind=kCustom, calls=%fused_computation.2 | custom fusion | flops 2621440 | bytes 31458560 | tf_op jit(solution)/shard_map/scatter-add | solution.py:46
  85.8 1.5 copy_bitcast_fusion.6
  87.3 13.3 %gather_fusion = bf16[320,64,128]{2,1,0:T(8,128)(2,1)} fusion(bf16[64,64,128]{2,0,1:T(8,128)(2,1)S(1)} %copy_bitcast_fusion.6, s32[1024]{0:T(1024)S(1)} %pad_clamp_fusion), kind=kCustom, calls=%fused_computation.clone | custom fusion | bytes 10487040 | tf_op jit(solution)/shard_map/jit(_take)/gather | solution.py:30
  100.7 11.0 %fusion.10 = bf16[64,8,8,128]{3,2,1,0:T(8,128)(2,1)} fusion(bf16[64,5,128,128]{3,2,1,0:T(8,128)(2,1)} %param.16, bf16[64,5,64,128]{3,2,1,0:T(8,128)(2,1)} %bitcast.181, pred[64,5]{1,0:T(8,128)(4,1)S(1)} %copy.44, bf16[64,5]{1,0:T(8,128)(2,1)S(1)} %get-tuple-element.6), kind=kOutput, calls=%fused_computation.24 | convolution fusion | flops 676855808 | bytes 16778176 | tf_op jit(solution)/shard_map/rsab,nrsb->nra/dot_general | solution.py:31
  111.7 2.5 copy.106
  115.7 50.0 %all-reduce.3.cloned.1.call-done = bf16[64,8192]{1,0:T(8,128)(2,1)} async-done(((bf16[64,8192]{1,0:T(8,128)(2,1)}), bf16[64,8192]{1,0:T(8,128)(2,1)}) %all-reduce.3.cloned.1.call-update) | async-done | bytes 1048592 | tf_op jit(solution)/shard_map/psum | solution.py:76
  165.7 2.0 fusion.44
  167.7 24.2 %psum.50 = f32[64,64]{0,1:T(8,128)S(1)} all-reduce(f32[64,64]{0,1:T(8,128)S(1)} %fusion.44), channel_id=1, replica_groups=mesh['row'=8,'col'=4] {'row'}, use_global_device_ids=true, to_apply=%region_1.3 | all-reduce | flops 4096 | bytes 32768 | tf_op jit(solution)/shard_map/psum | solution.py:77
  192.0 5.8 cholesky.74
  199.2 4.9 custom-call.15
  204.1 1.1 fusion.45
  205.3 39.4 %psum.51 = f32[64,64]{0,1:T(8,128)S(1)} all-reduce(f32[64,64]{0,1:T(8,128)S(1)} %fusion.45), channel_id=1, replica_groups=mesh['row'=8,'col'=4] {'row','col'}, use_global_device_ids=true, to_apply=%region_6.9 | all-reduce | flops 4096 | bytes 32768 | tf_op jit(solution)/shard_map/psum | solution.py:68
  245.1 2.3 convolution_subtract_fusion.1
  247.4 1.3 copy-done
  249.2 10.2 %broadcast_multiply_fusion.1 = f32[64,64,5,128]{3,1,2,0:T(8,128)} fusion(f32[64,5]{1,0:T(8,128)S(1)} %get-tuple-element.8, bf16[64,5,128,128]{3,2,1,0:T(8,128)(2,1)} %param.16, bf16[64,64,128,1]{2,1,0,3:T(8,128)(2,1)S(1)} %bitcast.183), kind=kOutput, calls=%fused_computation.14 | convolution fusion | flops 673710080 | bytes 22021376 | tf_op jit(solution)/shard_map/rsab,nra->rsnb/dot_general | solution.py:42
  259.6 33.0 %scatter_fusion.1 = f32[64,64,128]{2,1,0:T(8,128)S(1)} fusion(f32[64,64,128]{2,1,0:T(8,128)S(1)} %broadcast.76.clone.1, s32[320]{0:T(512)S(1)} %reshape.148, f32[320,64,128]{2,1,0:T(8,128)} %bitcast.179), kind=kCustom, calls=%fused_computation.3 | custom fusion | flops 2621440 | bytes 31458560 | tf_op jit(solution)/shard_map/scatter-add | solution.py:46
  293.9 5.8 cholesky.85
  301.1 4.9 custom-call.17
  306.0 24.8 %reduce-scatter.6.cloned.1.call-done = bf16[64,1024]{1,0:T(8,128)(2,1)} async-done(((bf16[64,8192]{1,0:T(8,128)(2,1)}), bf16[64,1024]{1,0:T(8,128)(2,1)}) %reduce-scatter.6.cloned.1.call-update) | async-done | bytes 131088 | tf_op jit(solution)/shard_map/reduce_scatter | solution.py:65
  330.8 1.1 fusion.46
  331.9 39.4 %psum.52 = f32[64,64]{0,1:T(8,128)S(1)} all-reduce(f32[64,64]{0,1:T(8,128)S(1)} %fusion.46), channel_id=1, replica_groups=mesh['row'=8,'col'=4] {'row','col'}, use_global_device_ids=true, to_apply=%region_9.14 | all-reduce | flops 4096 | bytes 32768 | tf_op jit(solution)/shard_map/psum | solution.py:68
  371.8 2.0 fusion.43
  374.1 24.0 %all-gather.8.cloned.1.call-done = bf16[64,8192]{1,0:T(8,128)(2,1)} async-done(((bf16[64,1024]{1,0:T(8,128)(2,1)}), bf16[64,8192]{1,0:T(8,128)(2,1)}) %all-gather.8.cloned.1.call-update) | async-done | bytes 1048592 | tf_op jit(solution)/shard_map/all_gather | solution.py:74
  398.1 1.5 copy_bitcast_fusion.5
  399.6 13.3 %gather_fusion.1 = bf16[320,64,128]{2,1,0:T(8,128)(2,1)} fusion(bf16[64,64,128]{2,0,1:T(8,128)(2,1)S(1)} %copy_bitcast_fusion.5, s32[1024]{0:T(1024)S(1)} %pad_clamp_fusion), kind=kCustom, calls=%fused_computation.1.clone | custom fusion | bytes 10487040 | tf_op jit(solution)/shard_map/jit(_take)/gather | solution.py:30
  412.9 11.0 %fusion.11 = bf16[64,8,8,128]{3,2,1,0:T(8,128)(2,1)} fusion(bf16[64,5,128,128]{3,2,1,0:T(8,128)(2,1)} %param.16, bf16[64,5,64,128]{3,2,1,0:T(8,128)(2,1)} %bitcast.180, pred[64,5]{1,0:T(8,128)(4,1)S(1)} %copy.44, bf16[64,5]{1,0:T(8,128)(2,1)S(1)} %get-tuple-element.6), kind=kOutput, calls=%fused_computation.25 | convolution fusion | flops 676855808 | bytes 16778176 | tf_op jit(solution)/shard_map/rsab,nrsb->nra/dot_general | solution.py:31
  424.0 2.6 copy.105
  426.6 52.0 %all-reduce.5.cloned.1.call-done = bf16[64,8192]{1,0:T(8,128)(2,1)} async-done(((bf16[64,8192]{1,0:T(8,128)(2,1)}), bf16[64,8192]{1,0:T(8,128)(2,1)}) %all-reduce.5.cloned.1.call-update) | async-done | bytes 1048592 | tf_op jit(solution)/shard_map/psum | solution.py:76
  478.6 2.0 fusion.47
  480.6 24.5 %psum.54 = f32[64,64]{0,1:T(8,128)S(1)} all-reduce(f32[64,64]{0,1:T(8,128)S(1)} %fusion.47), channel_id=1, replica_groups=mesh['row'=8,'col'=4] {'row'}, use_global_device_ids=true, to_apply=%region_11.16 | all-reduce | flops 4096 | bytes 32768 | tf_op jit(solution)/shard_map/psum | solution.py:77
  505.2 5.8 cholesky.96
  512.4 4.9 custom-call.19
  517.7 2.3 convolution_subtract_fusion
  520.0 1.3 copy-done.2
  521.8 10.2 %broadcast_multiply_fusion = f32[64,64,5,128]{3,1,2,0:T(8,128)} fusion(f32[64,5]{1,0:T(8,128)S(1)} %get-tuple-element.8, bf16[64,5,128,128]{3,2,1,0:T(8,128)(2,1)} %param.16, bf16[64,64,128,1]{2,1,0,3:T(8,128)(2,1)S(1)} %bitcast.182), kind=kOutput, calls=%fused_computation.13 | convolution fusion | flops 673710080 | bytes 22021376 | tf_op jit(solution)/shard_map/rsab,nra->rsnb/dot_general | solution.py:42
  532.2 33.0 %scatter_fusion.2 = f32[64,64,128]{2,1,0:T(8,128)S(1)} fusion(f32[64,64,128]{2,1,0:T(8,128)S(1)} %broadcast.76, s32[320]{0:T(512)S(1)} %reshape.148, f32[320,64,128]{2,1,0:T(8,128)} %bitcast.177), kind=kCustom, calls=%fused_computation.4 | custom fusion | flops 2621440 | bytes 31458560 | tf_op jit(solution)/shard_map/scatter-add | solution.py:46
  566.9 5.8 cholesky.107
  574.0 4.9 custom-call.21
  578.9 1.9 constant_dynamic-slice_fusion
  581.9 18.1 %reduce-scatter.8.cloned.1.call-done = bf16[64,1024]{1,0:T(8,128)(2,1)} async-done(((bf16[64,8192]{1,0:T(8,128)(2,1)}), bf16[64,1024]{1,0:T(8,128)(2,1)}) %reduce-scatter.8.cloned.1.call-update) | async-done | bytes 131088 | tf_op jit(solution)/shard_map/reduce_scatter | solution.py:65
  600.0 1.1 fusion.48
  601.2 39.4 %psum.55 = f32[64,64]{1,0:T(8,128)S(1)} all-reduce(f32[64,64]{1,0:T(8,128)S(1)} %fusion.48), channel_id=1, replica_groups=mesh['row'=8,'col'=4] {'row','col'}, use_global_device_ids=true, to_apply=%region_14.19 | all-reduce | flops 4096 | bytes 32768 | tf_op jit(solution)/shard_map/psum | solution.py:68
  641.0 2.0 convolution_add_fusion
  (77 shorter events, 18.0 us)
Async XLA Ops:
  7.2 33.7 %all-gather.6.cloned.1.call-start = ((), (), s32[]{:S(2)}) async-start(), calls=%async_computation.5 | async-start | bytes 1310720 | tf_op jit(solution)/shard_map/all_gather | solution.py:58
  9.0 76.8 %all-gather.4.cloned.1.call-start = ((), (), s32[]{:S(2)}) async-start(), calls=%async_computation.3 | async-start | bytes 1179648 | tf_op jit(solution)/shard_map/all_gather | solution.py:74
  10.7 155.0 %all-reduce.3.cloned.1.call-start = ((), (), s32[]{:S(2)}) async-start(), calls=%async_computation.4 | async-start | bytes 2097152 | tf_op jit(solution)/shard_map/psum | solution.py:76
  111.7 133.4 %copy-start.3 = (bf16[64,8192]{1,0:T(8,128)(2,1)S(1)}, bf16[64,8192]{1,0:T(8,128)(2,1)}, u32[]{:S(2)}) copy-start(bf16[64,8192]{1,0:T(8,128)(2,1)} %all-gather.6.cloned.1.call-done) | copy-start | bytes 3145732
  114.3 89.9 %reduce-scatter.4.cloned.1.call-start = ((), (), s32[]{:S(2)}) async-start(), calls=%async_computation.6 | async-start | bytes 1179648 | tf_op jit(solution)/shard_map/reduce_scatter | solution.py:65
  115.5 215.3 %reduce-scatter.6.cloned.1.call-start = ((), (), s32[]{:S(2)}) async-start(), calls=%async_computation.7 | async-start | bytes 1179648 | tf_op jit(solution)/shard_map/reduce_scatter | solution.py:65
  247.4 1.3 copy-start
  259.6 112.2 %copy-start.4 = (f32[64,1024]{1,0:T(8,128)S(1)}, f32[64,1024]{1,0:T(8,128)}, u32[]{:S(2)}) copy-start(f32[64,1024]{1,0:T(8,128)} %param.15) | copy-start | bytes 786436
  293.7 104.3 %all-gather.8.cloned.1.call-start = ((), (), s32[]{:S(2)}) async-start(), calls=%async_computation.8 | async-start | bytes 1179648 | tf_op jit(solution)/shard_map/all_gather | solution.py:74
  373.8 104.8 %all-reduce.5.cloned.1.call-start = ((), (), s32[]{:S(2)}) async-start(), calls=%async_computation.9 | async-start | bytes 2097152 | tf_op jit(solution)/shard_map/psum | solution.py:76
  424.0 93.7 %copy-start.1 = (f32[64,8192]{1,0:T(8,128)S(1)}, f32[64,8192]{1,0:T(8,128)}, u32[]{:S(2)}) copy-start(f32[64,8192]{1,0:T(8,128)} %copy-done) | copy-start | bytes 6291460
  426.6 173.4 %reduce-scatter.8.cloned.1.call-start = ((), (), s32[]{:S(2)}) async-start(), calls=%async_computation.10 | async-start | bytes 1179648 | tf_op jit(solution)/shard_map/reduce_scatter | solution.py:65
  520.0 1.3 copy-start.2
  532.2 34.2 %copy-start.5 = (f32[64,1024]{1,0:T(8,128)S(1)}, f32[64,1024]{1,0:T(8,128)}, u32[]{:S(2)}) copy-start(f32[64,1024]{1,0:T(8,128)} %param.13) | copy-start | bytes 786436
Sparse Core Ops, SparseCore 0:
  10.1 30.6 all-gather.5
  43.3 22.7 all-gather.3
  114.4 51.2 all-reduce.2
  168.7 35.3 reduce-scatter.3
  293.9 36.8 reduce-scatter.5
  373.9 24.0 all-gather.7
  426.7 51.8 all-reduce.4
  566.4 33.5 reduce-scatter.7
where the time goes:
time: 662 us; the launch traced here: 650 us
  waiting for transfers between devices  196 us (30%)
  blocking collectives  167 us (25%)
  other arithmetic  157 us (24%)
  matrix products  71.7 us (11%)
  local copies, waits for them, and re-layouts  43.6 us (7%)
  between operations  15 us (2%)
    psum x3, blocking collectives, gradient_step(): gamma_value = lax.psum(gram_matrix(gradient), ('row', 'col'))  118 us
    psum x2, waiting for transfers between devices, per_device(): lax.psum(image_partial_term.astype(jnp.bfloat16), 'col').astype(jnp.float32)  102 us
    scatter-add x3, other arithmetic, gradients(): jax.ops.segment_sum(contrib.reshape(-1, rhs_count, tile_width), tile_bloc...  99 us
    psum x2, blocking collectives, per_device(): curvature = lax.psum(gram_matrix(image), 'row')  48.7 us
    reduce_scatter x3, waiting for transfers between devices, gradient_step(): lax.psum_scatter(partial_term.astype(jnp.bfloat16), 'row', scatter_dimens...  43 us
    dot_general x3, matrix products, gradients(): jnp.einsum('rsab,nra->rsnb', jacobian_tiles, row_view, preferred_element_...  30.5 us
    all_gather x1, waiting for transfers between devices, per_device(): lax.all_gather(residual.astype(jnp.bfloat16), 'col', axis=1, tiled=True)  26.7 us
    gather x2, local copies, waits for them, and re-layouts, images(): jnp.take(table_view, tile_blocks, axis=1) * live_slot[None, :, :, None]  26.7 us
  transfers between devices with their start and end apart: 8, of which 7 were waited for; matrix products, arithmetic and copies ran while one was open for 14% of the time, Pallas kernels for 0%

commit v1 on v0

v1 whole, which is shorter than its diff:
```python
import functools

import jax
import jax.numpy as jnp
from jax import lax
from jax.experimental import pallas as pl
from jax.experimental.pallas import tpu as pltpu
from jax.sharding import PartitionSpec as P

CHUNK = 8


def times_highest(left, right):
    return jnp.dot(left, right, precision=lax.Precision.HIGHEST)


def gram_matrix(values):
    return lax.dot_general(
        values,
        values,
        (((1,), (1,)), ((), ())),
        precision=lax.Precision.HIGHEST,
        preferred_element_type=jnp.float32,
    )


def gram_half(values):
    return lax.dot_general(
        values, values, (((1,), (1,)), ((), ())), preferred_element_type=jnp.float32
    )


def solve_kernel(matrix_ref, right_ref, out_ref):
    size = matrix_ref.shape[0]
    work = jnp.concatenate([matrix_ref[...], right_ref[...]], axis=1)
    rows = lax.broadcasted_iota(jnp.int32, (size, 1), 0)
    for k in range(size):
        pivot_row = work[k : k + 1, :]
        column = work[:, k : k + 1]
        pivot = work[k : k + 1, k : k + 1]
        scaled = pivot_row / pivot
        work = jnp.where(rows == k, scaled, work - column * scaled)
    out_ref[...] = work[:, size:]


def solve_spd(matrix, right):
    return pl.pallas_call(
        solve_kernel,
        out_shape=jax.ShapeDtypeStruct(right.shape, jnp.float32),
        name="spd_solve",
    )(matrix, right)


def image_kernel(where_ref, *refs, shards, slots, blocks_per):
    table_refs = refs[:shards]
    tiles_ref, out_ref, table_ref = refs[shards:]
    step = pl.program_id(0)
    tile = tiles_ref.shape[-1]
    total = shards * blocks_per

    @pl.when(step == 0)
    def _():
        for shard in range(shards):
            table_ref[shard] = table_refs[shard][...]

    for local in range(CHUNK):
        pieces = []
        tiles = []
        for slot in range(slots):
            place = where_ref[(step * CHUNK + local) * slots + slot]
            live = place < total
            spot = jnp.where(live, place, 0)
            piece = table_ref[
                spot // blocks_per,
                :,
                pl.ds(pl.multiple_of((spot % blocks_per) * tile, tile), tile),
            ]
            pieces.append(jnp.where(live, piece, jnp.zeros_like(piece)))
            tiles.append(tiles_ref[local, slot])
        product = lax.dot_general(
            jnp.concatenate(pieces, axis=1),
            jnp.concatenate(tiles, axis=1),
            (((1,), (1,)), ((), ())),
            preferred_element_type=jnp.float32,
        )
        out_ref[:, local * tile : (local + 1) * tile] = product.astype(out_ref.dtype)


def images(where_to, table, tiles):
    sensors, slots, tile, _ = tiles.shape
    shards = len(table)
    rhs, width = table[0].shape
    grid_spec = pltpu.PrefetchScalarGridSpec(
        num_scalar_prefetch=1,
        grid=(sensors // CHUNK,),
        in_specs=[pl.BlockSpec((rhs, width), lambda i, w: (0, 0)) for _ in table]
        + [pl.BlockSpec((CHUNK, slots, tile, tile), lambda i, w: (i, 0, 0, 0))],
        out_specs=pl.BlockSpec((rhs, CHUNK * tile), lambda i, w: (0, i)),
        scratch_shapes=[pltpu.VMEM((shards, rhs, width), jnp.bfloat16)],
    )
    return pl.pallas_call(
        functools.partial(
            image_kernel, shards=shards, slots=slots, blocks_per=width // tile
        ),
        grid_spec=grid_spec,
        out_shape=jax.ShapeDtypeStruct((rhs, sensors * tile), jnp.bfloat16),
        name="images",
    )(where_to, *table, tiles)


def gradient_kernel(
    where_ref, rows_ref, tiles_ref, keep_ref, send_ref, sums_ref, *, slots, blocks_per
):
    step = pl.program_id(0)
    tile = tiles_ref.shape[-1]

    @pl.when(step == 0)
    def _():
        sums_ref[...] = jnp.zeros_like(sums_ref)

    for local in range(CHUNK):
        rows = rows_ref[:, local * tile : (local + 1) * tile]
        tiles = jnp.concatenate([tiles_ref[local, slot] for slot in range(slots)], axis=1)
        product = jnp.dot(rows, tiles, preferred_element_type=jnp.float32)
        spots = [where_ref[(step * CHUNK + local) * slots + slot] for slot in range(slots)]
        olds = [sums_ref[spot] for spot in spots]
        for slot in range(slots):
            sums_ref[spots[slot]] = (
                olds[slot] + product[:, slot * tile : (slot + 1) * tile]
            )

    @pl.when(step == pl.num_programs(0) - 1)
    def _():
        for shard in range(keep_ref.shape[0]):
            for block in range(blocks_per):
                span = slice(block * tile, (block + 1) * tile)
                keep_ref[shard, :, span] = sums_ref[2 * shard * blocks_per + block]
                send_ref[shard, :, span] = sums_ref[
                    (2 * shard + 1) * blocks_per + block
                ].astype(send_ref.dtype)


def gradients(where_to, rows, tiles, shards, width):
    sensors, slots, tile, _ = tiles.shape
    rhs = rows.shape[0]
    half = shards // 2
    grid_spec = pltpu.PrefetchScalarGridSpec(
        num_scalar_prefetch=1,
        grid=(sensors // CHUNK,),
        in_specs=[
            pl.BlockSpec((rhs, CHUNK * tile), lambda i, w: (0, i)),
            pl.BlockSpec((CHUNK, slots, tile, tile), lambda i, w: (i, 0, 0, 0)),
        ],
        out_specs=[
            pl.BlockSpec((half, rhs, width), lambda i, w: (0, 0, 0)),
            pl.BlockSpec((half, rhs, width), lambda i, w: (0, 0, 0)),
        ],
        scratch_shapes=[
            pltpu.VMEM((shards * width // tile + 1, rhs, tile), jnp.float32)
        ],
    )
    return pl.pallas_call(
        functools.partial(gradient_kernel, slots=slots, blocks_per=width // tile),
        grid_spec=grid_spec,
        out_shape=[
            jax.ShapeDtypeStruct((half, rhs, width), jnp.float32),
            jax.ShapeDtypeStruct((half, rhs, width), jnp.bfloat16),
        ],
        name="gradients",
    )(where_to, rows, tiles)


def per_device(
    solution, residual, direction, jacobian_tiles, tile_blocks, tile_counts, *, n_row, n_col
):
    rhs, width = direction.shape
    tile = jacobian_tiles.shape[2]
    slots = jacobian_tiles.shape[1]
    blocks_per = width // tile
    me = lax.axis_index("row")
    odd = (me & 1) == 1
    low, high = n_row // 4, n_row // 2

    def swap(value, mask, axis="row"):
        size = n_row if axis == "row" else n_col
        return lax.ppermute(value, axis, [(i, i ^ mask) for i in range(size)])

    def swap_mixed(value):
        return lax.ppermute(
            value, "row", [(i, i ^ (high if i & 1 else low)) for i in range(n_row)]
        )

    def sum_row(value):
        mask = 1
        while mask < n_row:
            value = value + swap(value, mask)
            mask *= 2
        return value

    def sum_all(value):
        value = sum_row(value)
        mask = 1
        while mask < n_col:
            value = value + swap(value, mask, "col")
            mask *= 2
        return value

    def gather_row(value):
        held = {0: value, low: swap(value, low), high: swap(value, high)}
        held[low | high] = swap_mixed(jnp.where(odd, held[low], held[high]))
        mask = low // 2
        while mask:
            for j in list(held):
                held[j ^ mask] = swap(held[j], mask)
            mask //= 2
        return [held[j] for j in range(n_row)]

    def scatter_row(parts):
        keep, send = parts
        got = swap(send, 1)
        held = {2 * j: keep[j] + got[j].astype(jnp.float32) for j in range(n_row // 2)}
        mask = 2
        while mask < low:
            for j in [j for j in held if j & mask]:
                moved = swap(held.pop(j).astype(jnp.bfloat16), mask)
                held[j ^ mask] = held[j ^ mask] + moved.astype(jnp.float32)
            mask *= 2
        cross = swap_mixed(held[low | high].astype(jnp.bfloat16)).astype(jnp.float32)
        to_low = (held[low] + jnp.where(odd, cross, 0.0)).astype(jnp.bfloat16)
        to_high = (held[high] + jnp.where(odd, 0.0, cross)).astype(jnp.bfloat16)
        return (
            held[0]
            + swap(to_low, low).astype(jnp.float32)
            + swap(to_high, high).astype(jnp.float32)
        )

    owner = (tile_blocks // blocks_per) ^ me
    live = jnp.arange(slots, dtype=jnp.int32)[None, :] < tile_counts
    where_to = jnp.where(
        live, owner * blocks_per + tile_blocks % blocks_per, n_row * blocks_per
    ).reshape(-1)

    def image_of(value):
        table = gather_row(value.astype(jnp.bfloat16))
        return lax.psum(images(where_to, table, jacobian_tiles), "col")

    def gradient_of(rows):
        return scatter_row(gradients(where_to, rows, jacobian_tiles, n_row, width))

    rows_half = lax.all_gather(residual.astype(jnp.bfloat16), "col", axis=1, tiled=True)
    image_first = image_of(direction)
    gradient = gradient_of(rows_half)
    gamma = sum_all(gram_matrix(gradient))

    curvature = sum_row(gram_half(image_first))
    change = gradient_of(image_first)
    alpha = solve_spd(curvature, gamma)
    gradient = gradient - times_highest(alpha.T, change)

    image_part = image_of(gradient)
    gamma_next = sum_all(gram_matrix(gradient))
    beta = solve_spd(gamma, gamma_next)
    image = image_part.astype(jnp.float32) + times_highest(
        beta.T, image_first.astype(jnp.float32)
    )
    iterate = solution + times_highest(alpha.T, direction)
    direction = gradient + times_highest(beta.T, direction)
    share_rows = residual.shape[1]
    start = lax.axis_index("col") * share_rows

    def share(value):
        return lax.dynamic_slice_in_dim(value, start, share_rows, 1).astype(jnp.float32)

    remaining = residual - times_highest(alpha.T, share(image_first))
    gamma = gamma_next

    image_half = image.astype(jnp.bfloat16)
    curvature = sum_row(gram_half(image_half))
    change = gradient_of(image_half)
    alpha = solve_spd(curvature, gamma)
    inverse = solve_spd(gamma, jnp.eye(rhs, dtype=jnp.float32))
    weighted = times_highest(inverse, direction)
    gradient = gradient - times_highest(alpha.T, change)
    gamma_next = sum_all(gram_matrix(gradient))
    iterate = iterate + times_highest(alpha.T, direction)
    remaining = remaining - times_highest(alpha.T, share(image))
    direction = gradient + times_highest(gamma_next, weighted)
    return (iterate, remaining, direction)


def solution(mesh):
    vector = P(None, ("row", "col"))
    placed = (
        vector,
        vector,
        vector,
        P("row", "col", None, None),
        P("row", "col"),
        P("row", "col"),
    )
    return jax.shard_map(
        functools.partial(per_device, n_row=mesh.shape["row"], n_col=mesh.shape["col"]),
        mesh=mesh,
        in_specs=placed,
        out_specs=(vector, vector, vector),
        check_vma=False,
    )
```

time: 662 us -> 299 us (0.45); the launches traced: 650 us -> 298 us
  blocking collectives: 167 us -> 0 us
  other arithmetic: 157 us -> 12.8 us
  Pallas kernels: 0 us -> 78.9 us
  waiting for transfers between devices: 196 us -> 133 us
  matrix products: 71.7 us -> 17 us
  local copies, waits for them, and re-layouts: 43.6 us -> 3.66 us
  starting transfers between devices: 0.72 us -> 38.2 us
    psum x5 -> x0, blocking collectives: 167 us -> none  [the longest x3 118 us: gradient_step(): gamma_value = lax.psum(gram_matrix(gradient), ('row', 'col'))]
    scatter-add x3 -> x0, other arithmetic: 99 us -> none  [gradients(): jax.ops.segment_sum(contrib.reshape(-1, rhs_count, tile_width), tile_bloc...]
    pallas_call x0 -> x9, Pallas kernels: none -> 78.9 us  [the longest x3 29.7 us: gradients(): pl.pallas_call(functools.partial(gradient_kernel, slots=slots, blocks_per...]
    ppermute x0 -> x47, waiting for transfers between devices: none -> 63.1 us  [the longest x42 50.3 us: swap(): return lax.ppermute(value, axis, [(i, i ^ mask) for i in range(size)])]
    dot_general x10 -> x5, matrix products: 59.9 us -> 3 us  [the longest x3 2.17 us: gram_matrix(): lax.dot_general(values, values, (((1,), (1,)), ((), ())), precision=lax.P...]
    another operation x20 -> x0, other arithmetic: 48.3 us -> none  [the longest x12 26.1 us: solve_spd(): factor_low = jnp.linalg.cholesky(matrix)]
    reduce_scatter x3 -> x0, waiting for transfers between devices: 43 us -> none  [gradient_step(): lax.psum_scatter(partial_term.astype(jnp.bfloat16), 'row', scatter_dimens...]
    ppermute x0 -> x47, starting transfers between devices: none -> 38.1 us  [the longest x42 33.6 us: swap(): return lax.ppermute(value, axis, [(i, i ^ mask) for i in range(size)])]
  transfers between devices with their start and end apart: 8 -> 50, of which waited for: 7 -> 31; matrix products, arithmetic and copies ran while one was open for 14% -> 7% of each run, Pallas kernels for 0% -> 20%
where the time goes in v1:
time: 299 us; the launch traced here: 298 us
  waiting for transfers between devices  133 us (44%)
  Pallas kernels  78.9 us (26%)
  starting transfers between devices  38.2 us (13%)
  matrix products  17 us (6%)
  between operations  14.2 us (5%)
  other arithmetic  12.8 us (4%)
  local copies, waits for them, and re-layouts  3.66 us (1%)
    psum x2, waiting for transfers between devices, image_of(): return lax.psum(images(where_to, table, jacobian_tiles), 'col')  65.7 us
    ppermute x42, waiting for transfers between devices, swap(): return lax.ppermute(value, axis, [(i, i ^ mask) for i in range(size)])  50.3 us
    ppermute x42, starting transfers between devices, swap(): return lax.ppermute(value, axis, [(i, i ^ mask) for i in range(size)])  33.6 us
    pallas_call x3, Pallas kernels, gradients(): pl.pallas_call(functools.partial(gradient_kernel, slots=slots, blocks_per...  29.7 us
    pallas_call x4, Pallas kernels, solve_spd(): pl.pallas_call(solve_kernel, out_shape=jax.ShapeDtypeStruct(right.shape,...  27.8 us
    pallas_call x2, Pallas kernels, images(): pl.pallas_call(functools.partial(image_kernel, shards=shards, slots=slots...  21.3 us
    dot_general x10, matrix products, times_highest(): return jnp.dot(left, right, precision=lax.Precision.HIGHEST)  14 us
    ppermute x5, waiting for transfers between devices, swap_mixed(): lax.ppermute(value, 'row', [(i, i ^ (high if i & 1 else low)) for i in ra...  12.9 us
  transfers between devices with their start and end apart: 50, of which 31 were waited for; matrix products, arithmetic and copies ran while one was open for 7% of the time, Pallas kernels for 20%

profile of v1, /device:TPU:0, one launch (start us, length us, event | category | flops | bytes accessed | tf_op | source)
XLA Modules:
  0.0 297.7 jit_solution(11068351195836940039)
XLA Ops:
  7.2 1.8 convert_element_type.132
  10.0 3.0 %collective-permute-start.1 = (bf16[64,1024]{1,0:T(8,128)(2,1)S(1)}, bf16[64,1024]{1,0:T(8,128)(2,1)S(1)}, u32[]{:S(2)}, u32[]{:S(2)}) collective-permute-start(bf16[64,1024]{1,0:T(8,128)(2,1)S(1)} %convert_element_type.131.refs_0_), channel_id=1, source_target_pairs={{0,8},{4,12},{8,0},{12,4},{16,24},{20,28},{24,16},{28,20},{1,9},{5... | collective-permute-start | bytes 393224 | tf_op jit(solution)/shard_map/ppermute | solution.py:186
  13.1 1.5 collective-permute-start.3
  14.6 2.0 collective-permute-done.1.refs_2_
  16.6 1.5 collective-permute-done.3.refs_4_
  19.0 4.1 %collective-permute-done.5.refs_6_ = bf16[64,1024]{1,0:T(8,128)(2,1)S(1)} collective-permute-done((bf16[64,1024]{1,0:T(8,128)(2,1)S(1)}, bf16[64,1024]{1,0:T(8,128)(2,1)S(1)}, u32[]{:S(2)}, u32[]{:S(2)}) %collective-permute-start.5) | collective-permute-done | bytes 131104 | tf_op jit(solution)/shard_map/ppermute | solution.py:189
  26.1 10.7 %images.2 = bf16[64,8192]{1,0:T(8,128)(2,1)} custom-call(s32[320]{0:T(512)} %reshape.36.where_ref, bf16[64,1024]{1,0:T(8,128)(2,1)} %copy-done.11, bf16[64,1024]{1,0:T(8,128)(2,1)} %copy-done.20, bf16[64,1024]{1,0:T(8,128)(2,1)} %copy-done.12, bf16[64,1024]{1,0:T(8,128)(2,1)} %copy-done.21, bf16[64,1024]{1,0:T(8,128)(2,1)} %copy-done.13, ...), custom_call_target="tpu_custom_call" | custom-call | tf_op jit(solution)/shard_map/images/pallas_call | solution.py:101
  36.8 4.1 %all-gather.2.cloned.1.call-done.rows_ref = bf16[64,8192]{1,0:T(8,128)(2,1)} async-done(((bf16[64,2048]{1,0:T(8,128)(2,1)}), bf16[64,8192]{1,0:T(8,128)(2,1)}) %all-gather.2.cloned.1.call-update) | async-done | bytes 1048592 | tf_op jit(solution)/shard_map/all_gather | solution.py:250
  40.9 9.9 %gradients.3 = (f32[4,64,1024]{2,1,0:T(8,128)}, bf16[4,64,1024]{2,1,0:T(8,128)(2,1)}) custom-call(s32[320]{0:T(512)} %reshape.36.where_ref, bf16[64,8192]{1,0:T(8,128)(2,1)} %all-gather.2.cloned.1.call-done.rows_ref, bf16[64,5,128,128]{3,2,1,0:T(8,128)(2,1)} %tiles_ref.5), custom_call_target="tpu_custom_call" | custom-call | tf_op jit(solution)/shard_map/gradients/pallas_call | solution.py:162
  50.7 43.8 %all-reduce.3.cloned.1.call-done.rows_ref = bf16[64,8192]{1,0:T(8,128)(2,1)} async-done(((bf16[64,8192]{1,0:T(8,128)(2,1)}), bf16[64,8192]{1,0:T(8,128)(2,1)}) %all-reduce.3.cloned.1.call-update) | async-done | bytes 1048592 | tf_op jit(solution)/shard_map/psum | solution.py:245
  94.5 9.9 %gradients.4 = (f32[4,64,1024]{2,1,0:T(8,128)}, bf16[4,64,1024]{2,1,0:T(8,128)(2,1)}) custom-call(s32[320]{0:T(512)} %reshape.36.where_ref, bf16[64,8192]{1,0:T(8,128)(2,1)} %all-reduce.3.cloned.1.call-done.rows_ref, bf16[64,5,128,128]{3,2,1,0:T(8,128)(2,1)} %tiles_ref.5), custom_call_target="tpu_custom_call" | custom-call | tf_op jit(solution)/shard_map/gradients/pallas_call | solution.py:162
  106.2 1.5 collective-permute-start.11
  107.7 3.5 %collective-permute-done.11 = bf16[64,1024]{1,0:T(8,128)(2,1)S(1)} collective-permute-done((bf16[64,1024]{1,0:T(8,128)(2,1)S(1)}, bf16[64,1024]{1,0:T(8,128)(2,1)S(1)}, u32[]{:S(2)}, u32[]{:S(2)}) %collective-permute-start.11) | collective-permute-done | bytes 131104 | tf_op jit(solution)/shard_map/ppermute | solution.py:189
  112.3 1.5 collective-permute-start.13
  113.9 1.5 collective-permute-start.12
  117.4 1.4 collective-permute-done.12
  118.8 1.4 fusion.49
  124.9 3.0 %collective-permute-done.15 = f32[64,64]{1,0:T(8,128)S(1)} collective-permute-done((f32[64,64]{1,0:T(8,128)S(1)}, f32[64,64]{1,0:T(8,128)S(1)}, u32[]{:S(2)}, u32[]{:S(2)}) %collective-permute-start.15) | collective-permute-done | bytes 16416 | tf_op jit(solution)/shard_map/ppermute | solution.py:186
  135.7 2.0 collective-permute-start.18
  138.3 2.2 collective-permute-done.18
  141.1 6.9 %spd_solve.4 = f32[64,64]{1,0:T(8,128)} custom-call(f32[64,64]{1,0:T(8,128)} %add.202.matrix_ref, f32[64,64]{1,0:T(8,128)} %add.218.right_ref.matrix_ref), custom_call_target="tpu_custom_call" | custom-call | tf_op jit(solution)/shard_map/spd_solve/pallas_call | solution.py:47
  148.1 1.6 fusion.52
  149.7 1.7 collective-permute-start.24
  152.3 2.5 collective-permute-done.24.refs_2_
  154.7 1.7 collective-permute-done.26.refs_4_
  157.4 4.1 %collective-permute-done.28.refs_6_ = bf16[64,1024]{1,0:T(8,128)(2,1)S(1)} collective-permute-done((bf16[64,1024]{1,0:T(8,128)(2,1)S(1)}, bf16[64,1024]{1,0:T(8,128)(2,1)S(1)}, u32[]{:S(2)}, u32[]{:S(2)}) %collective-permute-start.28) | collective-permute-done | bytes 131104 | tf_op jit(solution)/shard_map/ppermute | solution.py:189
  163.5 10.7 %images.3 = bf16[64,8192]{1,0:T(8,128)(2,1)} custom-call(s32[320]{0:T(512)} %reshape.36.where_ref, bf16[64,1024]{1,0:T(8,128)(2,1)} %copy-done.16, bf16[64,1024]{1,0:T(8,128)(2,1)} %copy-done.24, bf16[64,1024]{1,0:T(8,128)(2,1)} %copy-done.14, bf16[64,1024]{1,0:T(8,128)(2,1)} %copy-done.25, bf16[64,1024]{1,0:T(8,128)(2,1)} %copy-done.15, ...), custom_call_target="tpu_custom_call" | custom-call | tf_op jit(solution)/shard_map/images/pallas_call | solution.py:101
  176.2 3.6 %collective-permute-done.31 = f32[64,64]{1,0:T(8,128)S(1)} collective-permute-done((f32[64,64]{1,0:T(8,128)S(1)}, f32[64,64]{1,0:T(8,128)S(1)}, u32[]{:S(2)}, u32[]{:S(2)}) %collective-permute-start.31) | collective-permute-done | bytes 16416 | tf_op jit(solution)/shard_map/ppermute | solution.py:186
  180.7 3.0 collective-permute-done.32
  185.0 4.8 %collective-permute-done.33 = f32[64,64]{1,0:T(8,128)S(1)} collective-permute-done((f32[64,64]{1,0:T(8,128)S(1)}, f32[64,64]{1,0:T(8,128)S(1)}, u32[]{:S(2)}, u32[]{:S(2)}) %collective-permute-start.33) | collective-permute-done | bytes 16416 | tf_op jit(solution)/shard_map/ppermute | solution.py:186
  190.2 6.7 %collective-permute-done.34 = f32[64,64]{1,0:T(8,128)S(1)} collective-permute-done((f32[64,64]{1,0:T(8,128)S(1)}, f32[64,64]{1,0:T(8,128)S(1)}, u32[]{:S(2)}, u32[]{:S(2)}) %collective-permute-start.34) | collective-permute-done | bytes 16416 | tf_op jit(solution)/shard_map/ppermute | solution.py:186
  197.5 6.9 %spd_solve.5 = f32[64,64]{1,0:T(8,128)} custom-call(f32[64,64]{1,0:T(8,128)} %add.218.right_ref.matrix_ref, f32[64,64]{1,0:T(8,128)} %add.235.right_ref.matrix_ref), custom_call_target="tpu_custom_call" | custom-call | tf_op jit(solution)/shard_map/spd_solve/pallas_call | solution.py:47
  204.4 22.0 %all-reduce.5.cloned.1.call-done = bf16[64,8192]{1,0:T(8,128)(2,1)} async-done(((bf16[64,8192]{1,0:T(8,128)(2,1)}), bf16[64,8192]{1,0:T(8,128)(2,1)}) %all-reduce.5.cloned.1.call-update) | async-done | bytes 1048592 | tf_op jit(solution)/shard_map/psum | solution.py:245
  226.4 4.0 %fusion.51 = (bf16[64,8192]{1,0:T(8,128)(2,1)}, f32[64,8192]{1,0:T(8,128)}) fusion(bf16[64,8192]{1,0:T(8,128)(2,1)} %all-reduce.5.cloned.1.call-done, f32[64,64]{1,0:T(8,128)} %spd_solve.5, bf16[64,8192]{1,0:T(8,128)(2,1)S(1)} %copy-done), kind=kOutput, calls=%fused_computation.77 | convolution fusion | flops 404226048 | bytes 5259264 | tf_op jit(solution)/shard_map/dot_general | solution.py:14
  230.4 10.0 %gradients.5 = (f32[4,64,1024]{2,1,0:T(8,128)}, bf16[4,64,1024]{2,1,0:T(8,128)(2,1)}) custom-call(s32[320]{0:T(512)} %reshape.36.where_ref, bf16[64,8192]{1,0:T(8,128)(2,1)} %get-tuple-element.15.rows_ref, bf16[64,5,128,128]{3,2,1,0:T(8,128)(2,1)} %tiles_ref.5), custom_call_target="tpu_custom_call" | custom-call | tf_op jit(solution)/shard_map/gradients/pallas_call | solution.py:162
  240.4 2.1 collective-permute-done.38
  243.5 1.5 collective-permute-start.39
  248.4 2.3 collective-permute-done.36
  250.7 1.5 collective-permute-start.37
  252.2 1.8 fusion.13
  255.9 7.0 %spd_solve.7 = f32[64,64]{1,0:T(8,128)} custom-call(f32[64,64]{1,0:T(8,128)} %add.235.right_ref.matrix_ref, f32[64,64]{1,0:T(8,128)} %fusion.38.right_ref), custom_call_target="tpu_custom_call" | custom-call | tf_op jit(solution)/shard_map/spd_solve/pallas_call | solution.py:47
  263.5 6.9 %spd_solve.6 = f32[64,64]{1,0:T(8,128)} custom-call(f32[64,64]{1,0:T(8,128)} %add.239.matrix_ref, f32[64,64]{1,0:T(8,128)} %add.235.right_ref.matrix_ref), custom_call_target="tpu_custom_call" | custom-call | tf_op jit(solution)/shard_map/spd_solve/pallas_call | solution.py:47
  270.5 1.4 convolution_subtract_fusion.1
  274.6 1.7 fusion.2
  279.8 1.6 collective-permute-done.44
  283.2 2.2 collective-permute-done.45
  285.3 1.7 collective-permute-start.46
  288.2 2.0 collective-permute-done.46
  (171 shorter events, 49.6 us)
Async XLA Ops:
  7.2 33.7 %all-gather.2.cloned.1.call-start = ((), (), s32[]{:S(2)}) async-start(), calls=%async_computation.1 | async-start | bytes 1310720 | tf_op jit(solution)/shard_map/all_gather | solution.py:250
  9.0 85.5 %all-reduce.3.cloned.1.call-start = ((), (), s32[]{:S(2)}) async-start(), calls=%async_computation | async-start | bytes 2097152 | tf_op jit(solution)/shard_map/psum | solution.py:245
  10.0 6.5 %collective-permute-start.1 = (bf16[64,1024]{1,0:T(8,128)(2,1)S(1)}, bf16[64,1024]{1,0:T(8,128)(2,1)S(1)}, u32[]{:S(2)}, u32[]{:S(2)}) collective-permute-start(bf16[64,1024]{1,0:T(8,128)(2,1)S(1)} %convert_element_type.131.refs_0_), channel_id=1, source_target_pairs={{0,8},{4,12},{8,0},{12,4},{16,24},{20,28},{24,16},{28,20},{1,9},{5... | collective-permute-start | bytes 393224 | tf_op jit(solution)/shard_map/ppermute | solution.py:186
  13.1 5.0 %collective-permute-start.3 = (bf16[64,1024]{1,0:T(8,128)(2,1)S(1)}, bf16[64,1024]{1,0:T(8,128)(2,1)S(1)}, u32[]{:S(2)}, u32[]{:S(2)}) collective-permute-start(bf16[64,1024]{1,0:T(8,128)(2,1)S(1)} %convert_element_type.131.refs_0_), channel_id=1, source_target_pairs={{0,16},{4,20},{8,24},{12,28},{16,0},{20,4},{24,8},{28,12},{1,17},{... | collective-permute-start | bytes 393224 | tf_op jit(solution)/shard_map/ppermute | solution.py:186
  18.1 5.0 %collective-permute-start.5 = (bf16[64,1024]{1,0:T(8,128)(2,1)S(1)}, bf16[64,1024]{1,0:T(8,128)(2,1)S(1)}, u32[]{:S(2)}, u32[]{:S(2)}) collective-permute-start(bf16[64,1024]{1,0:T(8,128)(2,1)S(1)} %broadcast_select_fusion.1), channel_id=1, source_target_pairs={{0,8},{4,20},{8,0},{12,28},{16,24},{20,4},{24,16},{28,12},{1,9},{5... | collective-permute-start | bytes 393224 | tf_op jit(solution)/shard_map/ppermute | solution.py:189
  18.5 6.2 %collective-permute-start = (bf16[64,1024]{1,0:T(8,128)(2,1)S(1)}, bf16[64,1024]{1,0:T(8,128)(2,1)S(1)}, u32[]{:S(2)}, u32[]{:S(2)}) collective-permute-start(bf16[64,1024]{1,0:T(8,128)(2,1)S(1)} %convert_element_type.131.refs_0_), channel_id=1, source_target_pairs={{0,4},{4,0},{8,12},{12,8},{16,20},{20,16},{24,28},{28,24},{1,5},{5... | collective-permute-start | bytes 393224 | tf_op jit(solution)/shard_map/ppermute | solution.py:186
  18.5 6.2 %collective-permute-start.2 = (bf16[64,1024]{1,0:T(8,128)(2,1)S(1)}, bf16[64,1024]{1,0:T(8,128)(2,1)S(1)}, u32[]{:S(2)}, u32[]{:S(2)}) collective-permute-start(bf16[64,1024]{1,0:T(8,128)(2,1)S(1)} %collective-permute-done.1.refs_2_), channel_id=1, source_target_pairs={{0,4},{4,0},{8,12},{12,8},{16,20},{20,16},{24,28},{28,24},{1,5},{5... | collective-permute-start | bytes 393224 | tf_op jit(solution)/shard_map/ppermute | solution.py:186
  19.0 5.7 %collective-permute-start.4 = (bf16[64,1024]{1,0:T(8,128)(2,1)S(1)}, bf16[64,1024]{1,0:T(8,128)(2,1)S(1)}, u32[]{:S(2)}, u32[]{:S(2)}) collective-permute-start(bf16[64,1024]{1,0:T(8,128)(2,1)S(1)} %collective-permute-done.3.refs_4_), channel_id=1, source_target_pairs={{0,4},{4,0},{8,12},{12,8},{16,20},{20,16},{24,28},{28,24},{1,5},{5... | collective-permute-start | bytes 393224 | tf_op jit(solution)/shard_map/ppermute | solution.py:186
  23.1 1.6 collective-permute-start.6
  36.8 189.6 %all-reduce.5.cloned.1.call-start = ((), (), s32[]{:S(2)}) async-start(), calls=%async_computation.2 | async-start | bytes 2097152 | tf_op jit(solution)/shard_map/psum | solution.py:245
  50.7 53.6 %collective-permute-start.10 = (bf16[4,64,1024]{2,1,0:T(8,128)(2,1)}, bf16[4,64,1024]{2,1,0:T(8,128)(2,1)S(1)}, u32[]{:S(2)}, u32[]{:S(2)}) collective-permute-start(bf16[4,64,1024]{2,1,0:T(8,128)(2,1)} %get-tuple-element.10), channel_id=1, source_target_pairs={{0,4},{4,0},{8,12},{12,8},{16,20},{20,16},{24,28},{28,24},{1,5},{5... | collective-permute-start | bytes 1572872 | tf_op jit(solution)/shard_map/ppermute | solution.py:186
  104.4 10.9 %collective-permute-start.19 = (bf16[4,64,1024]{2,1,0:T(8,128)(2,1)}, bf16[4,64,1024]{2,1,0:T(8,128)(2,1)S(1)}, u32[]{:S(2)}, u32[]{:S(2)}) collective-permute-start(bf16[4,64,1024]{2,1,0:T(8,128)(2,1)} %get-tuple-element.12), channel_id=1, source_target_pairs={{0,4},{4,0},{8,12},{12,8},{16,20},{20,16},{24,28},{28,24},{1,5},{5... | collective-permute-start | bytes 1572872 | tf_op jit(solution)/shard_map/ppermute | solution.py:186
  106.2 5.0 %collective-permute-start.11 = (bf16[64,1024]{1,0:T(8,128)(2,1)S(1)}, bf16[64,1024]{1,0:T(8,128)(2,1)S(1)}, u32[]{:S(2)}, u32[]{:S(2)}) collective-permute-start(bf16[64,1024]{1,0:T(8,128)(2,1)S(1)} %fusion.32), channel_id=1, source_target_pairs={{0,8},{4,20},{8,0},{12,28},{16,24},{20,4},{24,16},{28,12},{1,9},{5... | collective-permute-start | bytes 393224 | tf_op jit(solution)/shard_map/ppermute | solution.py:189
  112.3 5.1 %collective-permute-start.13 = (bf16[64,1024]{1,0:T(8,128)(2,1)S(1)}, bf16[64,1024]{1,0:T(8,128)(2,1)S(1)}, u32[]{:S(2)}, u32[]{:S(2)}) collective-permute-start(bf16[64,1024]{1,0:T(8,128)(2,1)S(1)} %get-tuple-element.22), channel_id=1, source_target_pairs={{0,16},{4,20},{8,24},{12,28},{16,0},{20,4},{24,8},{28,12},{1,17},{... | collective-permute-start | bytes 393224 | tf_op jit(solution)/shard_map/ppermute | solution.py:186
  113.9 5.0 %collective-permute-start.12 = (bf16[64,1024]{1,0:T(8,128)(2,1)S(1)}, bf16[64,1024]{1,0:T(8,128)(2,1)S(1)}, u32[]{:S(2)}, u32[]{:S(2)}) collective-permute-start(bf16[64,1024]{1,0:T(8,128)(2,1)S(1)} %get-tuple-element.21), channel_id=1, source_target_pairs={{0,8},{4,12},{8,0},{12,4},{16,24},{20,28},{24,16},{28,20},{1,9},{5... | collective-permute-start | bytes 393224 | tf_op jit(solution)/shard_map/ppermute | solution.py:186
  116.5 5.0 %collective-permute-start.20 = (bf16[64,1024]{1,0:T(8,128)(2,1)S(1)}, bf16[64,1024]{1,0:T(8,128)(2,1)S(1)}, u32[]{:S(2)}, u32[]{:S(2)}) collective-permute-start(bf16[64,1024]{1,0:T(8,128)(2,1)S(1)} %fusion.33), channel_id=1, source_target_pairs={{0,8},{4,20},{8,0},{12,28},{16,24},{20,4},{24,16},{28,12},{1,9},{5... | collective-permute-start | bytes 393224 | tf_op jit(solution)/shard_map/ppermute | solution.py:189
  120.3 2.9 collective-permute-start.14
  121.6 26.4 %collective-permute-start.22 = (bf16[64,1024]{1,0:T(8,128)(2,1)S(1)}, bf16[64,1024]{1,0:T(8,128)(2,1)}, u32[]{:S(2)}, u32[]{:S(2)}) collective-permute-start(bf16[64,1024]{1,0:T(8,128)(2,1)S(1)} %get-tuple-element.20), channel_id=1, source_target_pairs={{0,16},{4,20},{8,24},{12,28},{16,0},{20,4},{24,8},{28,12},{1,17},{... | collective-permute-start | bytes 393224 | tf_op jit(solution)/shard_map/ppermute | solution.py:186
  122.3 25.8 %collective-permute-start.21 = (bf16[64,1024]{1,0:T(8,128)(2,1)S(1)}, bf16[64,1024]{1,0:T(8,128)(2,1)}, u32[]{:S(2)}, u32[]{:S(2)}) collective-permute-start(bf16[64,1024]{1,0:T(8,128)(2,1)S(1)} %get-tuple-element.19), channel_id=1, source_target_pairs={{0,8},{4,12},{8,0},{12,4},{16,24},{20,28},{24,16},{28,20},{1,9},{5... | collective-permute-start | bytes 393224 | tf_op jit(solution)/shard_map/ppermute | solution.py:186
  123.2 4.7 %collective-permute-start.15 = (f32[64,64]{1,0:T(8,128)S(1)}, f32[64,64]{1,0:T(8,128)S(1)}, u32[]{:S(2)}, u32[]{:S(2)}) collective-permute-start(f32[64,64]{1,0:T(8,128)S(1)} %add.214), channel_id=1, source_target_pairs={{0,8},{4,12},{8,0},{12,4},{16,24},{20,28},{24,16},{28,20},{1,9},{5... | collective-permute-start | bytes 49160 | tf_op jit(solution)/shard_map/ppermute | solution.py:186
  124.8 4.3 %collective-permute-start.7 = (f32[64,64]{1,0:T(8,128)S(1)}, f32[64,64]{1,0:T(8,128)S(1)}, u32[]{:S(2)}, u32[]{:S(2)}) collective-permute-start(f32[64,64]{1,0:T(8,128)S(1)} %fusion.53), channel_id=1, source_target_pairs={{0,4},{4,0},{8,12},{12,8},{16,20},{20,16},{24,28},{28,24},{1,5},{5... | collective-permute-start | bytes 49160 | tf_op jit(solution)/shard_map/ppermute | solution.py:186
  127.9 3.9 %collective-permute-start.16 = (f32[64,64]{1,0:T(8,128)S(1)}, f32[64,64]{1,0:T(8,128)S(1)}, u32[]{:S(2)}, u32[]{:S(2)}) collective-permute-start(f32[64,64]{1,0:T(8,128)S(1)} %add.215), channel_id=1, source_target_pairs={{0,16},{4,20},{8,24},{12,28},{16,0},{20,4},{24,8},{28,12},{1,17},{... | collective-permute-start | bytes 49160 | tf_op jit(solution)/shard_map/ppermute | solution.py:186
  129.1 4.1 %collective-permute-start.8 = (f32[64,64]{1,0:T(8,128)S(1)}, f32[64,64]{1,0:T(8,128)S(1)}, u32[]{:S(2)}, u32[]{:S(2)}) collective-permute-start(f32[64,64]{1,0:T(8,128)S(1)} %add.200), channel_id=1, source_target_pairs={{0,8},{4,12},{8,0},{12,4},{16,24},{20,28},{24,16},{28,20},{1,9},{5... | collective-permute-start | bytes 49160 | tf_op jit(solution)/shard_map/ppermute | solution.py:186
  131.8 3.9 %collective-permute-start.17 = (f32[64,64]{1,0:T(8,128)S(1)}, f32[64,64]{1,0:T(8,128)S(1)}, u32[]{:S(2)}, u32[]{:S(2)}) collective-permute-start(f32[64,64]{1,0:T(8,128)S(1)} %add.216), channel_id=1, source_target_pairs={{0,1},{1,0},{2,3},{3,2},{4,5},{5,4},{6,7},{7,6},{8,9},{9,8},{10,11... | collective-permute-start | bytes 49160 | tf_op jit(solution)/shard_map/ppermute | solution.py:186
  133.1 4.6 %collective-permute-start.9 = (f32[64,64]{1,0:T(8,128)S(1)}, f32[64,64]{1,0:T(8,128)S(1)}, u32[]{:S(2)}, u32[]{:S(2)}) collective-permute-start(f32[64,64]{1,0:T(8,128)S(1)} %add.201), channel_id=1, source_target_pairs={{0,16},{4,20},{8,24},{12,28},{16,0},{20,4},{24,8},{28,12},{1,17},{... | collective-permute-start | bytes 49160 | tf_op jit(solution)/shard_map/ppermute | solution.py:186
  135.7 4.8 %collective-permute-start.18 = (f32[64,64]{1,0:T(8,128)S(1)}, f32[64,64]{1,0:T(8,128)S(1)}, u32[]{:S(2)}, u32[]{:S(2)}) collective-permute-start(f32[64,64]{1,0:T(8,128)S(1)} %add.217), channel_id=1, source_target_pairs={{0,2},{1,3},{2,0},{3,1},{4,6},{5,7},{6,4},{7,5},{8,10},{9,11},{10,... | collective-permute-start | bytes 49160 | tf_op jit(solution)/shard_map/ppermute | solution.py:186
  149.7 5.0 %collective-permute-start.24 = (bf16[64,1024]{1,0:T(8,128)(2,1)S(1)}, bf16[64,1024]{1,0:T(8,128)(2,1)S(1)}, u32[]{:S(2)}, u32[]{:S(2)}) collective-permute-start(bf16[64,1024]{1,0:T(8,128)(2,1)S(1)} %get-tuple-element.23.refs_0_), channel_id=1, source_target_pairs={{0,8},{4,12},{8,0},{12,4},{16,24},{20,28},{24,16},{28,20},{1,9},{5... | collective-permute-start | bytes 393224 | tf_op jit(solution)/shard_map/ppermute | solution.py:186
  151.4 5.1 %collective-permute-start.26 = (bf16[64,1024]{1,0:T(8,128)(2,1)S(1)}, bf16[64,1024]{1,0:T(8,128)(2,1)S(1)}, u32[]{:S(2)}, u32[]{:S(2)}) collective-permute-start(bf16[64,1024]{1,0:T(8,128)(2,1)S(1)} %get-tuple-element.23.refs_0_), channel_id=1, source_target_pairs={{0,16},{4,20},{8,24},{12,28},{16,0},{20,4},{24,8},{28,12},{1,17},{... | collective-permute-start | bytes 393224 | tf_op jit(solution)/shard_map/ppermute | solution.py:186
  156.4 5.0 %collective-permute-start.28 = (bf16[64,1024]{1,0:T(8,128)(2,1)S(1)}, bf16[64,1024]{1,0:T(8,128)(2,1)S(1)}, u32[]{:S(2)}, u32[]{:S(2)}) collective-permute-start(bf16[64,1024]{1,0:T(8,128)(2,1)S(1)} %broadcast_select_fusion), channel_id=1, source_target_pairs={{0,8},{4,20},{8,0},{12,28},{16,24},{20,4},{24,16},{28,12},{1,9},{5... | collective-permute-start | bytes 393224 | tf_op jit(solution)/shard_map/ppermute | solution.py:189
  156.9 4.6 %collective-permute-start.23 = (bf16[64,1024]{1,0:T(8,128)(2,1)S(1)}, bf16[64,1024]{1,0:T(8,128)(2,1)S(1)}, u32[]{:S(2)}, u32[]{:S(2)}) collective-permute-start(bf16[64,1024]{1,0:T(8,128)(2,1)S(1)} %get-tuple-element.23.refs_0_), channel_id=1, source_target_pairs={{0,4},{4,0},{8,12},{12,8},{16,20},{20,16},{24,28},{28,24},{1,5},{5... | collective-permute-start | bytes 393224 | tf_op jit(solution)/shard_map/ppermute | solution.py:186
  156.9 4.6 %collective-permute-start.25 = (bf16[64,1024]{1,0:T(8,128)(2,1)S(1)}, bf16[64,1024]{1,0:T(8,128)(2,1)S(1)}, u32[]{:S(2)}, u32[]{:S(2)}) collective-permute-start(bf16[64,1024]{1,0:T(8,128)(2,1)S(1)} %collective-permute-done.24.refs_2_), channel_id=1, source_target_pairs={{0,4},{4,0},{8,12},{12,8},{16,20},{20,16},{24,28},{28,24},{1,5},{5... | collective-permute-start | bytes 393224 | tf_op jit(solution)/shard_map/ppermute | solution.py:186
  157.4 4.1 %collective-permute-start.27 = (bf16[64,1024]{1,0:T(8,128)(2,1)S(1)}, bf16[64,1024]{1,0:T(8,128)(2,1)S(1)}, u32[]{:S(2)}, u32[]{:S(2)}) collective-permute-start(bf16[64,1024]{1,0:T(8,128)(2,1)S(1)} %collective-permute-done.26.refs_4_), channel_id=1, source_target_pairs={{0,4},{4,0},{8,12},{12,8},{16,20},{20,16},{24,28},{28,24},{1,5},{5... | collective-permute-start | bytes 393224 | tf_op jit(solution)/shard_map/ppermute | solution.py:186
  161.5 1.3 collective-permute-start.29
  174.6 1.3 collective-permute-start.30
  175.8 3.9 %collective-permute-start.31 = (f32[64,64]{1,0:T(8,128)S(1)}, f32[64,64]{1,0:T(8,128)S(1)}, u32[]{:S(2)}, u32[]{:S(2)}) collective-permute-start(f32[64,64]{1,0:T(8,128)S(1)} %add.231), channel_id=1, source_target_pairs={{0,8},{4,12},{8,0},{12,4},{16,24},{20,28},{24,16},{28,20},{1,9},{5... | collective-permute-start | bytes 49160 | tf_op jit(solution)/shard_map/ppermute | solution.py:186
  179.8 3.9 %collective-permute-start.32 = (f32[64,64]{1,0:T(8,128)S(1)}, f32[64,64]{1,0:T(8,128)S(1)}, u32[]{:S(2)}, u32[]{:S(2)}) collective-permute-start(f32[64,64]{1,0:T(8,128)S(1)} %add.232), channel_id=1, source_target_pairs={{0,16},{4,20},{8,24},{12,28},{16,0},{20,4},{24,8},{28,12},{1,17},{... | collective-permute-start | bytes 49160 | tf_op jit(solution)/shard_map/ppermute | solution.py:186
  183.7 6.2 %collective-permute-start.33 = (f32[64,64]{1,0:T(8,128)S(1)}, f32[64,64]{1,0:T(8,128)S(1)}, u32[]{:S(2)}, u32[]{:S(2)}) collective-permute-start(f32[64,64]{1,0:T(8,128)S(1)} %add.233), channel_id=1, source_target_pairs={{0,1},{1,0},{2,3},{3,2},{4,5},{5,4},{6,7},{7,6},{8,9},{9,8},{10,11... | collective-permute-start | bytes 49160 | tf_op jit(solution)/shard_map/ppermute | solution.py:186
  189.9 7.0 %collective-permute-start.34 = (f32[64,64]{1,0:T(8,128)S(1)}, f32[64,64]{1,0:T(8,128)S(1)}, u32[]{:S(2)}, u32[]{:S(2)}) collective-permute-start(f32[64,64]{1,0:T(8,128)S(1)} %add.234), channel_id=1, source_target_pairs={{0,2},{1,3},{2,0},{3,1},{4,6},{5,7},{6,4},{7,5},{8,10},{9,11},{10,... | collective-permute-start | bytes 49160 | tf_op jit(solution)/shard_map/ppermute | solution.py:186
  240.4 2.1 collective-permute-start.38
  243.5 8.6 %collective-permute-start.39 = (bf16[64,1024]{1,0:T(8,128)(2,1)S(1)}, bf16[64,1024]{1,0:T(8,128)(2,1)S(1)}, u32[]{:S(2)}, u32[]{:S(2)}) collective-permute-start(bf16[64,1024]{1,0:T(8,128)(2,1)S(1)} %fusion.34), channel_id=1, source_target_pairs={{0,8},{4,20},{8,0},{12,28},{16,24},{20,4},{24,16},{28,12},{1,9},{5... | collective-permute-start | bytes 393224 | tf_op jit(solution)/shard_map/ppermute | solution.py:189
  246.8 3.9 %collective-permute-start.36 = (f32[64,64]{1,0:T(8,128)S(1)}, f32[64,64]{1,0:T(8,128)S(1)}, u32[]{:S(2)}, u32[]{:S(2)}) collective-permute-start(f32[64,64]{1,0:T(8,128)S(1)} %add.237), channel_id=1, source_target_pairs={{0,8},{4,12},{8,0},{12,4},{16,24},{20,28},{24,16},{28,20},{1,9},{5... | collective-permute-start | bytes 49160 | tf_op jit(solution)/shard_map/ppermute | solution.py:186
  250.7 12.2 %collective-permute-start.37 = (f32[64,64]{1,0:T(8,128)S(1)}, f32[64,64]{1,0:T(8,128)S(1)}, u32[]{:S(2)}, u32[]{:S(2)}) collective-permute-start(f32[64,64]{1,0:T(8,128)S(1)} %add.238), channel_id=1, source_target_pairs={{0,16},{4,20},{8,24},{12,28},{16,0},{20,4},{24,8},{28,12},{1,17},{... | collective-permute-start | bytes 49160 | tf_op jit(solution)/shard_map/ppermute | solution.py:186
  253.9 16.5 %collective-permute-start.41 = (bf16[64,1024]{1,0:T(8,128)(2,1)}, bf16[64,1024]{1,0:T(8,128)(2,1)S(1)}, u32[]{:S(2)}, u32[]{:S(2)}) collective-permute-start(bf16[64,1024]{1,0:T(8,128)(2,1)} %get-tuple-element.18), channel_id=1, source_target_pairs={{0,16},{4,20},{8,24},{12,28},{16,0},{20,4},{24,8},{28,12},{1,17},{... | collective-permute-start | bytes 393224 | tf_op jit(solution)/shard_map/ppermute | solution.py:186
  254.5 16.0 %collective-permute-start.40 = (bf16[64,1024]{1,0:T(8,128)(2,1)S(1)}, bf16[64,1024]{1,0:T(8,128)(2,1)S(1)}, u32[]{:S(2)}, u32[]{:S(2)}) collective-permute-start(bf16[64,1024]{1,0:T(8,128)(2,1)S(1)} %get-tuple-element.17), channel_id=1, source_target_pairs={{0,8},{4,12},{8,0},{12,4},{16,24},{20,28},{24,16},{28,20},{1,9},{5... | collective-permute-start | bytes 393224 | tf_op jit(solution)/shard_map/ppermute | solution.py:186
  273.5 3.9 %collective-permute-start.43 = (f32[64,64]{1,0:T(8,128)S(1)}, f32[64,64]{1,0:T(8,128)S(1)}, u32[]{:S(2)}, u32[]{:S(2)}) collective-permute-start(f32[64,64]{1,0:T(8,128)S(1)} %add.254), channel_id=1, source_target_pairs={{0,8},{4,12},{8,0},{12,4},{16,24},{20,28},{24,16},{28,20},{1,9},{5... | collective-permute-start | bytes 49160 | tf_op jit(solution)/shard_map/ppermute | solution.py:186
  277.5 3.9 %collective-permute-start.44 = (f32[64,64]{1,0:T(8,128)S(1)}, f32[64,64]{1,0:T(8,128)S(1)}, u32[]{:S(2)}, u32[]{:S(2)}) collective-permute-start(f32[64,64]{1,0:T(8,128)S(1)} %add.255), channel_id=1, source_target_pairs={{0,16},{4,20},{8,24},{12,28},{16,0},{20,4},{24,8},{28,12},{1,17},{... | collective-permute-start | bytes 49160 | tf_op jit(solution)/shard_map/ppermute | solution.py:186
  281.4 3.9 %collective-permute-start.45 = (f32[64,64]{1,0:T(8,128)S(1)}, f32[64,64]{1,0:T(8,128)S(1)}, u32[]{:S(2)}, u32[]{:S(2)}) collective-permute-start(f32[64,64]{1,0:T(8,128)S(1)} %add.256), channel_id=1, source_target_pairs={{0,1},{1,0},{2,3},{3,2},{4,5},{5,4},{6,7},{7,6},{8,9},{9,8},{10,11... | collective-permute-start | bytes 49160 | tf_op jit(solution)/shard_map/ppermute | solution.py:186
  285.3 4.8 %collective-permute-start.46 = (f32[64,64]{1,0:T(8,128)S(1)}, f32[64,64]{1,0:T(8,128)S(1)}, u32[]{:S(2)}, u32[]{:S(2)}) collective-permute-start(f32[64,64]{1,0:T(8,128)S(1)} %add.257), channel_id=1, source_target_pairs={{0,2},{1,3},{2,0},{3,1},{4,6},{5,7},{6,4},{7,5},{8,10},{9,11},{10,... | collective-permute-start | bytes 49160 | tf_op jit(solution)/shard_map/ppermute | solution.py:186
  (31 other events, 278.4 us)
Sparse Core Ops, SparseCore 0:
  10.1 30.6 all-gather.1
  43.2 51.2 all-reduce.2
  174.3 52.0 all-reduce.4

commit v2 on v0

v2 whole, which is shorter than its diff:
```python
import functools

import jax
import jax.numpy as jnp
from jax import lax
from jax.experimental import pallas as pl
from jax.experimental.pallas import tpu as pltpu
from jax.sharding import PartitionSpec as P

UNROLL = 8
IN_VMEM = pl.BlockSpec(memory_space=pltpu.VMEM)
IN_SMEM = pl.BlockSpec(memory_space=pltpu.SMEM)
PARAMS = pltpu.CompilerParams(vmem_limit_bytes=24 * 2**20)


def times_highest(left, right):
    return jnp.dot(left, right, precision=lax.Precision.HIGHEST)


def gram_matrix(values):
    return lax.dot_general(
        values,
        values,
        (((1,), (1,)), ((), ())),
        precision=lax.Precision.HIGHEST,
        preferred_element_type=jnp.float32,
    )


def solve_kernel(matrix_ref, right_ref, out_ref):
    size = matrix_ref.shape[0]
    work = jnp.concatenate([matrix_ref[...], right_ref[...]], axis=1)
    rows = lax.broadcasted_iota(jnp.int32, (size, 1), 0)
    for k in range(size):
        scaled = work[k : k + 1, :] / work[k : k + 1, k : k + 1]
        work = jnp.where(rows == k, scaled, work - work[:, k : k + 1] * scaled)
    out_ref[...] = work[:, size:]


def solve_spd(matrix, right):
    return pl.pallas_call(
        solve_kernel,
        out_shape=jax.ShapeDtypeStruct(right.shape, jnp.float32),
        name="spd_solve",
    )(matrix, right)


def tile_span(index, tile):
    return pl.ds(pl.multiple_of(index * tile, tile), tile)


def image_kernel(place_ref, start_ref, *refs, parts, first):
    table_refs = refs[: len(refs) - parts - 1 - first]
    tiles_ref = refs[len(table_refs)]
    out_refs = refs[len(table_refs) + 1 + first :]
    if first:
        table_ref = refs[len(table_refs) + 1]
        for shard, shard_ref in enumerate(table_refs):
            table_ref[shard] = shard_ref[...]
    else:
        table_ref = table_refs[0]
    slots, tile = tiles_ref.shape[1], tiles_ref.shape[2]
    blocks_per = table_ref.shape[2] // tile
    total = table_ref.shape[0] * blocks_per

    for part, out_ref in enumerate(out_refs):
        sensors = out_ref.shape[1] // tile
        unroll = min(UNROLL, sensors)

        def some(step, carry, part=part, out_ref=out_ref, unroll=unroll):
            for local in range(unroll):
                near = step * unroll + local
                sensor = start_ref[part] + near
                pieces, tiles = [], []
                for slot in range(slots):
                    place = place_ref[sensor * slots + slot]
                    live = place < total
                    spot = jnp.where(live, place, 0)
                    piece = table_ref[
                        spot // blocks_per, :, tile_span(spot % blocks_per, tile)
                    ]
                    pieces.append(jnp.where(live, piece, jnp.zeros_like(piece)))
                    tiles.append(tiles_ref[sensor, slot])
                product = lax.dot_general(
                    jnp.concatenate(tiles, axis=1),
                    jnp.concatenate(pieces, axis=1),
                    (((1,), (1,)), ((), ())),
                    preferred_element_type=jnp.float32,
                )
                out_ref[:, tile_span(near, tile)] = product.T.astype(out_ref.dtype)
            return carry

        lax.fori_loop(0, sensors // unroll, some, 0)


def images(place, starts, table, tiles, dtypes, count):
    parts = starts.shape[0]
    first = isinstance(table, list)
    shards = table if first else [table]
    rhs, width = shards[0].shape[-2:]
    sensors, slots, tile, _ = tiles.shape
    columns = sensors // count * tile
    out = [jax.ShapeDtypeStruct((rhs, columns), dtype) for dtype in dtypes]
    if first:
        out = [jax.ShapeDtypeStruct((len(shards), rhs, width), jnp.bfloat16)] + out
    return pl.pallas_call(
        functools.partial(image_kernel, parts=parts, first=first),
        in_specs=[IN_SMEM, IN_SMEM] + [IN_VMEM] * (len(shards) + 1),
        out_specs=[IN_VMEM] * len(out),
        out_shape=out,
        compiler_params=PARAMS,
        name="images",
    )(place, starts, *shards, tiles)


def gradient_kernel(place_ref, start_ref, *refs, parts, first):
    row_refs = refs[:parts]
    tiles_ref = refs[parts]
    if first:
        sums_ref = refs[parts + 1]
        sums_ref[...] = jnp.zeros_like(sums_ref)
    else:
        sums_ref, keep_ref, send_ref = refs[parts + 2 :]
    slots, tile = tiles_ref.shape[1], tiles_ref.shape[2]

    for part, row_ref in enumerate(row_refs):
        sensors = row_ref.shape[1] // tile
        unroll = min(UNROLL, sensors)

        def some(step, carry, part=part, row_ref=row_ref, unroll=unroll):
            for local in range(unroll):
                near = step * unroll + local
                sensor = start_ref[part] + near
                tiles = [tiles_ref[sensor, slot] for slot in range(slots)]
                product = jnp.dot(
                    row_ref[:, tile_span(near, tile)],
                    jnp.concatenate(tiles, axis=1),
                    preferred_element_type=jnp.float32,
                )
                spots = [place_ref[sensor * slots + slot] for slot in range(slots)]
                olds = [sums_ref[spot] for spot in spots]
                for slot in range(slots):
                    sums_ref[spots[slot]] = (
                        olds[slot] + product[:, slot * tile : (slot + 1) * tile]
                    )
            return carry

        lax.fori_loop(0, sensors // unroll, some, 0)

    if not first:
        blocks_per = keep_ref.shape[2] // tile
        for shard in range(keep_ref.shape[0]):
            for block in range(blocks_per):
                span = slice(block * tile, (block + 1) * tile)
                keep_ref[shard, :, span] = sums_ref[2 * shard * blocks_per + block]
                send_ref[shard, :, span] = sums_ref[
                    (2 * shard + 1) * blocks_per + block
                ].astype(send_ref.dtype)


def gradients_first(place, starts, rows, tiles, blocks):
    rhs, tile = rows[0].shape[0], tiles.shape[2]
    return pl.pallas_call(
        functools.partial(gradient_kernel, parts=len(rows), first=True),
        in_specs=[IN_SMEM, IN_SMEM] + [IN_VMEM] * (len(rows) + 1),
        out_specs=IN_VMEM,
        out_shape=jax.ShapeDtypeStruct((blocks + 1, rhs, tile), jnp.float32),
        compiler_params=PARAMS,
        name="gradients_first",
    )(place, starts, *rows, tiles)


def gradients_last(place, starts, rows, tiles, sums, shards, width):
    rhs = rows[0].shape[0]
    half = (shards // 2, rhs, width)
    _, keep, send = pl.pallas_call(
        functools.partial(gradient_kernel, parts=len(rows), first=False),
        in_specs=[IN_SMEM, IN_SMEM] + [IN_VMEM] * (len(rows) + 2),
        out_specs=[IN_VMEM] * 3,
        out_shape=[
            jax.ShapeDtypeStruct(sums.shape, jnp.float32),
            jax.ShapeDtypeStruct(half, jnp.float32),
            jax.ShapeDtypeStruct(half, jnp.bfloat16),
        ],
        input_output_aliases={len(rows) + 3: 0},
        compiler_params=PARAMS,
        name="gradients_last",
    )(place, starts, *rows, tiles, sums)
    return keep, send


def per_device(
    solution, residual, direction, jacobian_tiles, tile_blocks, tile_counts, *, n_row, n_col
):
    rhs, width = direction.shape
    sensors, slots, tile, _ = jacobian_tiles.shape
    blocks_per = width // tile
    my_row = lax.axis_index("row")
    my_col = lax.axis_index("col")
    chips = range(2, n_row, 2)
    far = range(n_col - 1, 1, -1)

    def swap_row(value, mask):
        return lax.ppermute(value, "row", [(i, i ^ mask) for i in range(n_row)])

    def swap_col(value, mask):
        return lax.ppermute(value, "col", [(i, i ^ mask) for i in range(n_col)])

    def add_up(values):
        while len(values) > 1:
            values = [a + b for a, b in zip(values[::2], values[1::2])] + (
                values[-1:] if len(values) % 2 else []
            )
        return values[0]

    def sum_row(value):
        value = value + swap_row(value, 1)
        return add_up([value] + [swap_row(value, mask) for mask in chips])

    def sum_all(value):
        value = sum_row(value)
        return add_up([value] + [swap_col(value, mask) for mask in range(1, n_col)])

    def gather_row(value):
        held = {0: value}
        for mask in chips:
            held[mask] = swap_row(value, mask)
        for mask in list(held):
            held[mask ^ 1] = swap_row(held[mask], 1)
        return [held[j] for j in range(n_row)]

    def scatter_row(parts):
        keep, send = parts
        got = swap_row(send, 1)
        held = [keep[j] + got[j].astype(jnp.float32) for j in range(n_row // 2)]
        moved = [swap_row(held[m // 2].astype(jnp.bfloat16), m) for m in chips]
        return add_up([held[0]] + [value.astype(jnp.float32) for value in moved])

    owner = (tile_blocks // blocks_per) ^ my_row
    live = jnp.arange(slots, dtype=jnp.int32)[None, :] < tile_counts
    place = jnp.where(
        live, owner * blocks_per + tile_blocks % blocks_per, n_row * blocks_per
    ).reshape(-1)
    starts = (my_col ^ jnp.arange(n_col, dtype=jnp.int32)) * (sensors // n_col)
    far_starts = starts[:1:-1]
    near_starts = starts[1::-1]

    def image_share(value):
        shards = gather_row(value.astype(jnp.bfloat16))
        table, *parts = images(
            place, far_starts, shards, jacobian_tiles, [jnp.bfloat16] * len(far), n_col
        )
        parts = [swap_col(part, mask) for part, mask in zip(parts, far)]
        next_part, own = images(
            place, near_starts, table, jacobian_tiles, [jnp.bfloat16, jnp.float32], n_col
        )
        parts = [own, swap_col(next_part, 1)] + parts
        return add_up([part.astype(jnp.float32) for part in parts])

    def gradient_of(share):
        half = share.astype(jnp.bfloat16)
        away = [swap_col(half, mask) for mask in far]
        sums = gradients_first(
            place, near_starts, [swap_col(half, 1), half], jacobian_tiles, n_row * blocks_per
        )
        return scatter_row(
            gradients_last(place, far_starts, away, jacobian_tiles, sums, n_row, width)
        )

    image_first = image_share(direction)
    gradient = gradient_of(residual)
    gamma = sum_all(gram_matrix(gradient))

    curvature = sum_all(gram_matrix(image_first))
    change = gradient_of(image_first)
    alpha = solve_spd(curvature, gamma)
    gradient = gradient - times_highest(alpha.T, change)

    image_part = image_share(gradient)
    gamma_next = sum_all(gram_matrix(gradient))
    beta = solve_spd(gamma, gamma_next)
    image = image_part + times_highest(beta.T, image_first)
    iterate = solution + times_highest(alpha.T, direction)
    direction = gradient + times_highest(beta.T, direction)
    remaining = residual - times_highest(alpha.T, image_first)
    gamma = gamma_next

    curvature = sum_all(gram_matrix(image))
    change = gradient_of(image)
    alpha = solve_spd(curvature, gamma)
    inverse = solve_spd(gamma, jnp.eye(rhs, dtype=jnp.float32))
    weighted = times_highest(inverse, direction)
    gradient = gradient - times_highest(alpha.T, change)
    gamma_next = sum_all(gram_matrix(gradient))
    iterate = iterate + times_highest(alpha.T, direction)
    remaining = remaining - times_highest(alpha.T, image)
    direction = gradient + times_highest(gamma_next, weighted)
    return (iterate, remaining, direction)


def solution(mesh):
    vector = P(None, ("row", "col"))
    placed = (
        vector,
        vector,
        vector,
        P("row", "col", None, None),
        P("row", "col"),
        P("row", "col"),
    )
    return jax.shard_map(
        functools.partial(per_device, n_row=mesh.shape["row"], n_col=mesh.shape["col"]),
        mesh=mesh,
        in_specs=placed,
        out_specs=(vector, vector, vector),
        check_vma=False,
    )
```

time: 662 us -> 263 us (0.40); the launches traced: 650 us -> 262 us
  blocking collectives: 167 us -> 0 us
  other arithmetic: 157 us -> 8.19 us
  waiting for transfers between devices: 196 us -> 77.9 us
  starting transfers between devices: 0.72 us -> 83.8 us
  matrix products: 71.7 us -> 14.3 us
  Pallas kernels: 0 us -> 54.5 us
  local copies, waits for them, and re-layouts: 43.6 us -> 21.9 us
  between operations: 15 us -> 1.28 us
    psum x5 -> x0, blocking collectives: 167 us -> none  [the longest x3 118 us: gradient_step(): gamma_value = lax.psum(gram_matrix(gradient), ('row', 'col'))]
    psum x2 -> x0, waiting for transfers between devices: 102 us -> none  [per_device(): lax.psum(image_partial_term.astype(jnp.bfloat16), 'col').astype(jnp.float32)]
    scatter-add x3 -> x0, other arithmetic: 99 us -> none  [gradients(): jax.ops.segment_sum(contrib.reshape(-1, rhs_count, tile_width), tile_bloc...]
    ppermute x0 -> x76, starting transfers between devices: none -> 83.8 us  [the longest x30 43 us: swap_col(): return lax.ppermute(value, 'col', [(i, i ^ mask) for i in range(n_col)])]
    ppermute x0 -> x76, waiting for transfers between devices: none -> 77.9 us  [the longest x30 59.1 us: swap_col(): return lax.ppermute(value, 'col', [(i, i ^ mask) for i in range(n_col)])]
    dot_general x10 -> x5, matrix products: 59.9 us -> 2.29 us  [gram_matrix(): lax.dot_general(values, values, (((1,), (1,)), ((), ())), precision=lax.P...]
    pallas_call x0 -> x14, Pallas kernels: none -> 54.5 us  [the longest x4 27.8 us: solve_spd(): pl.pallas_call(solve_kernel, out_shape=jax.ShapeDtypeStruct(right.shape,...]
    all_gather x3 -> x0, waiting for transfers between devices: 50.7 us -> none  [the longest x1 26.7 us: per_device(): lax.all_gather(residual.astype(jnp.bfloat16), 'col', axis=1, tiled=True)]
  transfers between devices with their start and end apart: 8 -> 76, of which waited for: 7 -> 22; matrix products, arithmetic and copies ran while one was open for 14% -> 6% of each run, Pallas kernels for 0% -> 21%
where the time goes in v2:
time: 263 us; the launch traced here: 262 us
  starting transfers between devices  83.8 us (32%)
  waiting for transfers between devices  77.9 us (30%)
  Pallas kernels  54.5 us (21%)
  local copies, waits for them, and re-layouts  21.9 us (8%)
  matrix products  14.3 us (5%)
  other arithmetic  8.19 us (3%)
    ppermute x30, waiting for transfers between devices, swap_col(): return lax.ppermute(value, 'col', [(i, i ^ mask) for i in range(n_col)])  59.1 us
    ppermute x30, starting transfers between devices, swap_col(): return lax.ppermute(value, 'col', [(i, i ^ mask) for i in range(n_col)])  43 us
    ppermute x46, starting transfers between devices, swap_row(): return lax.ppermute(value, 'row', [(i, i ^ mask) for i in range(n_row)])  40.7 us
    pallas_call x4, Pallas kernels, solve_spd(): pl.pallas_call(solve_kernel, out_shape=jax.ShapeDtypeStruct(right.shape,...  27.8 us
    unnamed x40, local copies, waits for them, and re-layouts  21.4 us
    ppermute x46, waiting for transfers between devices, swap_row(): return lax.ppermute(value, 'row', [(i, i ^ mask) for i in range(n_row)])  18.8 us
    pallas_call x4, Pallas kernels, images(): pl.pallas_call(functools.partial(image_kernel, parts=parts, first=first),...  13.1 us
    dot_general x10, matrix products, times_highest(): return jnp.dot(left, right, precision=lax.Precision.HIGHEST)  12 us
  transfers between devices with their start and end apart: 76, of which 22 were waited for; matrix products, arithmetic and copies ran while one was open for 6% of the time, Pallas kernels for 21%

profile of v2, /device:TPU:0, one launch (start us, length us, event | category | flops | bytes accessed | tf_op | source)
XLA Modules:
  0.0 261.8 jit_solution(3263928344081532512)
XLA Ops:
  1.6 3.0 %collective-permute-start.1 = (bf16[64,1024]{1,0:T(8,128)(2,1)S(1)}, bf16[64,1024]{1,0:T(8,128)(2,1)S(1)}, u32[]{:S(2)}, u32[]{:S(2)}) collective-permute-start(bf16[64,1024]{1,0:T(8,128)(2,1)S(1)} %convert_element_type.165.refs_0_), channel_id=1, source_target_pairs={{0,8},{4,12},{8,0},{12,4},{16,24},{20,28},{24,16},{28,20},{1,9},{5... | collective-permute-start | bytes 393224 | tf_op jit(solution)/shard_map/ppermute | solution.py:204
  7.3 2.1 collective-permute-start.19
  10.6 1.8 collective-permute-done.3.refs_4_
  13.2 3.6 %collective-permute-start.17 = (bf16[64,2048]{1,0:T(8,128)(2,1)S(1)}, bf16[64,2048]{1,0:T(8,128)(2,1)S(1)}, u32[]{:S(2)}, u32[]{:S(2)}) collective-permute-start(bf16[64,2048]{1,0:T(8,128)(2,1)S(1)} %convert_element_type.169.refs_1_), channel_id=1, source_target_pairs={{0,3},{1,2},{2,1},{3,0},{4,7},{5,6},{6,5},{7,4},{8,11},{9,10},{10,... | collective-permute-start | bytes 786440 | tf_op jit(solution)/shard_map/ppermute | solution.py:207
  16.8 4.0 %copy-done = bf16[64,5,128,128]{3,2,1,0:T(8,128)(2,1)S(1)} copy-done((bf16[64,5,128,128]{3,2,1,0:T(8,128)(2,1)S(1)}, bf16[64,5,128,128]{3,2,1,0:T(8,128)(2,1)}, u32[]{:S(2)}) %copy-start) | copy-done | bytes 10485784
  20.8 3.3 %images.4 = (bf16[8,64,1024]{2,1,0:T(8,128)(2,1)S(1)}, bf16[64,2048]{1,0:T(8,128)(2,1)S(1)}, bf16[64,2048]{1,0:T(8,128)(2,1)S(1)}) custom-call(s32[320]{0:T(512)S(1)} %reshape.42.place_ref, s32[2]{0:T(128)S(1)} %rev.7.start_ref, bf16[64,1024]{1,0:T(8,128)(2,1)S(1)} %convert_element_type.165.refs_0_, bf16[64,1024]{1,0:T(8,128)(2,1)S(1)} %collective-permute-done.refs_1_, ...), custom_call_target="tpu_custom_call" | custom-call | tf_op jit(solution)/shard_map/images/pallas_call | solution.py:106
  24.8 3.2 %images.5 = (bf16[64,2048]{1,0:T(8,128)(2,1)S(1)}, f32[64,2048]{1,0:T(8,128)S(1)}) custom-call(s32[320]{0:T(512)S(1)} %reshape.42.place_ref, s32[2]{0:T(128)S(1)} %rev.6.start_ref, bf16[8,64,1024]{2,1,0:T(8,128)(2,1)S(1)} %get-tuple-element.19.refs_0_, bf16[64,5,128,128]{3,2,1,0:T(8,128)(2,1)S(1)} %copy-done.1), custom_call_target="tpu_custom_call" | custom-call | tf_op jit(solution)/shard_map/images/pallas_call | solution.py:106
  28.8 3.6 %collective-permute-start.8 = (bf16[64,2048]{1,0:T(8,128)(2,1)S(1)}, bf16[64,2048]{1,0:T(8,128)(2,1)S(1)}, u32[]{:S(2)}, u32[]{:S(2)}) collective-permute-start(bf16[64,2048]{1,0:T(8,128)(2,1)S(1)} %get-tuple-element.22), channel_id=1, source_target_pairs={{0,3},{1,2},{2,1},{3,0},{4,7},{5,6},{6,5},{7,4},{8,11},{9,10},{10,... | collective-permute-start | bytes 786440 | tf_op jit(solution)/shard_map/ppermute | solution.py:207
  32.4 2.2 gradients_first.3.refs_3_
  34.6 16.9 %collective-permute-done.18.refs_1_ = bf16[64,2048]{1,0:T(8,128)(2,1)S(1)} collective-permute-done((bf16[64,2048]{1,0:T(8,128)(2,1)S(1)}, bf16[64,2048]{1,0:T(8,128)(2,1)S(1)}, u32[]{:S(2)}, u32[]{:S(2)}) %collective-permute-start.18) | collective-permute-done | bytes 262176 | tf_op jit(solution)/shard_map/ppermute | solution.py:207
  51.5 2.2 gradients_last.3
  53.9 7.9 %collective-permute-done.9 = bf16[64,2048]{1,0:T(8,128)(2,1)S(1)} collective-permute-done((bf16[64,2048]{1,0:T(8,128)(2,1)S(1)}, bf16[64,2048]{1,0:T(8,128)(2,1)S(1)}, u32[]{:S(2)}, u32[]{:S(2)}) %collective-permute-start.9) | collective-permute-done | bytes 262176 | tf_op jit(solution)/shard_map/ppermute | solution.py:207
  62.0 2.5 collective-permute-start.31
  68.8 5.5 %collective-permute-done.33.refs_0_ = bf16[64,2048]{1,0:T(8,128)(2,1)S(1)} collective-permute-done((bf16[64,2048]{1,0:T(8,128)(2,1)S(1)}, bf16[64,2048]{1,0:T(8,128)(2,1)S(1)}, u32[]{:S(2)}, u32[]{:S(2)}) %collective-permute-start.33) | collective-permute-done | bytes 262176 | tf_op jit(solution)/shard_map/ppermute | solution.py:207
  75.8 2.2 gradients_first.4.refs_3_
  79.6 7.8 %collective-permute-done.32.refs_1_ = bf16[64,2048]{1,0:T(8,128)(2,1)S(1)} collective-permute-done((bf16[64,2048]{1,0:T(8,128)(2,1)S(1)}, bf16[64,2048]{1,0:T(8,128)(2,1)S(1)}, u32[]{:S(2)}, u32[]{:S(2)}) %collective-permute-start.32) | collective-permute-done | bytes 262176 | tf_op jit(solution)/shard_map/ppermute | solution.py:207
  88.9 2.4 gradients_last.4
  91.3 1.7 collective-permute-start.13
  94.1 2.1 collective-permute-done.13
  96.3 3.0 %collective-permute-start.15 = (f32[64,64]{1,0:T(8,128)S(1)}, f32[64,64]{1,0:T(8,128)S(1)}, u32[]{:S(2)}, u32[]{:S(2)}) collective-permute-start(f32[64,64]{1,0:T(8,128)S(1)} %add_add_fusion.10), channel_id=1, source_target_pairs={{0,2},{1,3},{2,0},{3,1},{4,6},{5,7},{6,4},{7,5},{8,10},{9,11},{10,... | collective-permute-start | bytes 49160 | tf_op jit(solution)/shard_map/ppermute | solution.py:207
  101.3 1.7 collective-permute-start.26
  105.6 2.2 collective-permute-done.27
  108.0 2.9 %collective-permute-start.29 = (f32[64,64]{1,0:T(8,128)S(1)}, f32[64,64]{1,0:T(8,128)S(1)}, u32[]{:S(2)}, u32[]{:S(2)}) collective-permute-start(f32[64,64]{1,0:T(8,128)S(1)} %add_add_fusion.8), channel_id=1, source_target_pairs={{0,2},{1,3},{2,0},{3,1},{4,6},{5,7},{6,4},{7,5},{8,10},{9,11},{10,... | collective-permute-start | bytes 49160 | tf_op jit(solution)/shard_map/ppermute | solution.py:207
  117.9 6.9 %spd_solve.4 = f32[64,64]{1,0:T(8,128)} custom-call(f32[64,64]{1,0:T(8,128)} %add_add_fusion.9.matrix_ref, f32[64,64]{1,0:T(8,128)} %add_add_fusion.7.right_ref.matrix_ref), custom_call_target="tpu_custom_call" | custom-call | tf_op jit(solution)/shard_map/spd_solve/pallas_call | solution.py:41
  133.6 2.1 collective-permute-done.49
  137.9 2.5 collective-permute-done.51
  140.6 3.0 %collective-permute-start.53 = (f32[64,64]{1,0:T(8,128)S(1)}, f32[64,64]{1,0:T(8,128)S(1)}, u32[]{:S(2)}, u32[]{:S(2)}) collective-permute-start(f32[64,64]{1,0:T(8,128)S(1)} %add_add_fusion.6), channel_id=1, source_target_pairs={{0,2},{1,3},{2,0},{3,1},{4,6},{5,7},{6,4},{7,5},{8,10},{9,11},{10,... | collective-permute-start | bytes 49160 | tf_op jit(solution)/shard_map/ppermute | solution.py:207
  145.0 4.0 %copy-done.2 = bf16[64,5,128,128]{3,2,1,0:T(8,128)(2,1)S(1)} copy-done((bf16[64,5,128,128]{3,2,1,0:T(8,128)(2,1)S(1)}, bf16[64,5,128,128]{3,2,1,0:T(8,128)(2,1)}, u32[]{:S(2)}) %copy-start.2) | copy-done | bytes 10485784
  148.9 3.3 %images.6 = (bf16[8,64,1024]{2,1,0:T(8,128)(2,1)S(1)}, bf16[64,2048]{1,0:T(8,128)(2,1)S(1)}, bf16[64,2048]{1,0:T(8,128)(2,1)S(1)}) custom-call(s32[320]{0:T(512)S(1)} %reshape.42.place_ref, s32[2]{0:T(128)S(1)} %rev.7.start_ref, bf16[64,1024]{1,0:T(8,128)(2,1)S(1)} %get-tuple-element.50.refs_0_, bf16[64,1024]{1,0:T(8,128)(2,1)S(1)} %collective-permute-done.38.refs_1_, ...), custom_call_target="tpu_custom_call" | custom-call | tf_op jit(solution)/shard_map/images/pallas_call | solution.py:106
  152.2 4.0 %copy-done.3 = bf16[64,5,128,128]{3,2,1,0:T(8,128)(2,1)S(1)} copy-done((bf16[64,5,128,128]{3,2,1,0:T(8,128)(2,1)S(1)}, bf16[64,5,128,128]{3,2,1,0:T(8,128)(2,1)}, u32[]{:S(2)}) %copy-start.3) | copy-done | bytes 10485784
  156.2 3.4 %images.7 = (bf16[64,2048]{1,0:T(8,128)(2,1)S(1)}, f32[64,2048]{1,0:T(8,128)S(1)}) custom-call(s32[320]{0:T(512)S(1)} %reshape.42.place_ref, s32[2]{0:T(128)S(1)} %rev.6.start_ref, bf16[8,64,1024]{2,1,0:T(8,128)(2,1)S(1)} %get-tuple-element.28.refs_0_, bf16[64,5,128,128]{3,2,1,0:T(8,128)(2,1)S(1)} %copy-done.3), custom_call_target="tpu_custom_call" | custom-call | tf_op jit(solution)/shard_map/images/pallas_call | solution.py:106
  159.6 2.5 collective-permute-start.46
  163.8 6.9 %spd_solve.5 = f32[64,64]{1,0:T(8,128)} custom-call(f32[64,64]{1,0:T(8,128)} %add_add_fusion.7.right_ref.matrix_ref, f32[64,64]{1,0:T(8,128)} %add_add_fusion.5.right_ref.matrix_ref), custom_call_target="tpu_custom_call" | custom-call | tf_op jit(solution)/shard_map/spd_solve/pallas_call | solution.py:41
  172.1 1.9 collective-permute-done.46
  174.0 8.9 %collective-permute-done.47 = bf16[64,2048]{1,0:T(8,128)(2,1)S(1)} collective-permute-done((bf16[64,2048]{1,0:T(8,128)(2,1)S(1)}, bf16[64,2048]{1,0:T(8,128)(2,1)S(1)}, u32[]{:S(2)}, u32[]{:S(2)}) %collective-permute-start.47) | collective-permute-done | bytes 262176 | tf_op jit(solution)/shard_map/ppermute | solution.py:207
  183.1 2.5 collective-permute-start.62
  190.6 4.0 %collective-permute-done.64.refs_0_ = bf16[64,2048]{1,0:T(8,128)(2,1)S(1)} collective-permute-done((bf16[64,2048]{1,0:T(8,128)(2,1)S(1)}, bf16[64,2048]{1,0:T(8,128)(2,1)S(1)}, u32[]{:S(2)}, u32[]{:S(2)}) %collective-permute-start.64) | collective-permute-done | bytes 262176 | tf_op jit(solution)/shard_map/ppermute | solution.py:207
  197.3 6.9 %spd_solve.7 = f32[64,64]{1,0:T(8,128)} custom-call(f32[64,64]{1,0:T(8,128)} %add_add_fusion.5.right_ref.matrix_ref, f32[64,64]{1,0:T(8,128)} %fusion.35.right_ref), custom_call_target="tpu_custom_call" | custom-call | tf_op jit(solution)/shard_map/spd_solve/pallas_call | solution.py:41
  204.3 4.0 %copy-done.4 = bf16[64,5,128,128]{3,2,1,0:T(8,128)(2,1)S(1)} copy-done((bf16[64,5,128,128]{3,2,1,0:T(8,128)(2,1)S(1)}, bf16[64,5,128,128]{3,2,1,0:T(8,128)(2,1)}, u32[]{:S(2)}) %copy-start.4) | copy-done | bytes 10485784
  208.3 2.2 gradients_first.5.refs_3_
  210.5 4.0 %copy-done.5 = bf16[64,5,128,128]{3,2,1,0:T(8,128)(2,1)S(1)} copy-done((bf16[64,5,128,128]{3,2,1,0:T(8,128)(2,1)S(1)}, bf16[64,5,128,128]{3,2,1,0:T(8,128)(2,1)}, u32[]{:S(2)}) %copy-start.5) | copy-done | bytes 10485784
  214.5 2.5 gradients_last.5
  217.7 3.9 %collective-permute-start.61 = (f32[64,64]{1,0:T(8,128)S(1)}, f32[64,64]{1,0:T(8,128)S(1)}, u32[]{:S(2)}, u32[]{:S(2)}) collective-permute-start(f32[64,64]{1,0:T(8,128)S(1)} %add_add_fusion.4), channel_id=1, source_target_pairs={{0,3},{1,2},{2,1},{3,0},{4,7},{5,6},{6,5},{7,4},{8,11},{9,10},{10,... | collective-permute-start | bytes 49160 | tf_op jit(solution)/shard_map/ppermute | solution.py:207
  224.4 6.9 %spd_solve.6 = f32[64,64]{1,0:T(8,128)} custom-call(f32[64,64]{1,0:T(8,128)} %add_add_fusion.3.matrix_ref, f32[64,64]{1,0:T(8,128)} %add_add_fusion.5.right_ref.matrix_ref), custom_call_target="tpu_custom_call" | custom-call | tf_op jit(solution)/shard_map/spd_solve/pallas_call | solution.py:41
  238.6 2.1 collective-permute-done.67
  249.0 2.1 collective-permute-done.72
  251.7 3.3 %collective-permute-start.74 = (f32[64,64]{1,0:T(8,128)S(1)}, f32[64,64]{1,0:T(8,128)S(1)}, u32[]{:S(2)}, u32[]{:S(2)}) collective-permute-start(f32[64,64]{1,0:T(8,128)S(1)} %add_add_fusion.2), channel_id=1, source_target_pairs={{0,2},{1,3},{2,0},{3,1},{4,6},{5,7},{6,4},{7,5},{8,10},{9,11},{10,... | collective-permute-start | bytes 49160 | tf_op jit(solution)/shard_map/ppermute | solution.py:207
  256.9 3.8 %collective-permute-done.75 = f32[64,64]{1,0:T(8,128)S(1)} collective-permute-done((f32[64,64]{1,0:T(8,128)S(1)}, f32[64,64]{1,0:T(8,128)S(1)}, u32[]{:S(2)}, u32[]{:S(2)}) %collective-permute-start.75) | collective-permute-done | bytes 16416 | tf_op jit(solution)/shard_map/ppermute | solution.py:207
  (202 shorter events, 75.0 us)
Async XLA Ops:
  1.6 8.7 %collective-permute-start.1 = (bf16[64,1024]{1,0:T(8,128)(2,1)S(1)}, bf16[64,1024]{1,0:T(8,128)(2,1)S(1)}, u32[]{:S(2)}, u32[]{:S(2)}) collective-permute-start(bf16[64,1024]{1,0:T(8,128)(2,1)S(1)} %convert_element_type.165.refs_0_), channel_id=1, source_target_pairs={{0,8},{4,12},{8,0},{12,4},{16,24},{20,28},{24,16},{28,20},{1,9},{5... | collective-permute-start | bytes 393224 | tf_op jit(solution)/shard_map/ppermute | solution.py:204
  4.6 7.8 %collective-permute-start.3 = (bf16[64,1024]{1,0:T(8,128)(2,1)S(1)}, bf16[64,1024]{1,0:T(8,128)(2,1)S(1)}, u32[]{:S(2)}, u32[]{:S(2)}) collective-permute-start(bf16[64,1024]{1,0:T(8,128)(2,1)S(1)} %convert_element_type.165.refs_0_), channel_id=1, source_target_pairs={{0,16},{4,20},{8,24},{12,28},{16,0},{20,4},{24,8},{28,12},{1,17},{... | collective-permute-start | bytes 393224 | tf_op jit(solution)/shard_map/ppermute | solution.py:204
  6.2 7.0 %collective-permute-start = (bf16[64,1024]{1,0:T(8,128)(2,1)S(1)}, bf16[64,1024]{1,0:T(8,128)(2,1)S(1)}, u32[]{:S(2)}, u32[]{:S(2)}) collective-permute-start(bf16[64,1024]{1,0:T(8,128)(2,1)S(1)} %convert_element_type.165.refs_0_), channel_id=1, source_target_pairs={{0,4},{4,0},{8,12},{12,8},{16,20},{20,16},{24,28},{28,24},{1,5},{5... | collective-permute-start | bytes 393224 | tf_op jit(solution)/shard_map/ppermute | solution.py:204
  7.3 25.1 %collective-permute-start.19 = (bf16[64,2048]{1,0:T(8,128)(2,1)S(1)}, bf16[64,2048]{1,0:T(8,128)(2,1)S(1)}, u32[]{:S(2)}, u32[]{:S(2)}) collective-permute-start(bf16[64,2048]{1,0:T(8,128)(2,1)S(1)} %convert_element_type.169.refs_1_), channel_id=1, source_target_pairs={{0,1},{1,0},{2,3},{3,2},{4,5},{5,4},{6,7},{7,6},{8,9},{9,8},{10,11... | collective-permute-start | bytes 786440 | tf_op jit(solution)/shard_map/ppermute | solution.py:207
  10.3 6.5 %collective-permute-start.2 = (bf16[64,1024]{1,0:T(8,128)(2,1)S(1)}, bf16[64,1024]{1,0:T(8,128)(2,1)S(1)}, u32[]{:S(2)}, u32[]{:S(2)}) collective-permute-start(bf16[64,1024]{1,0:T(8,128)(2,1)S(1)} %collective-permute-done.1.refs_2_), channel_id=1, source_target_pairs={{0,4},{4,0},{8,12},{12,8},{16,20},{20,16},{24,28},{28,24},{1,5},{5... | collective-permute-start | bytes 393224 | tf_op jit(solution)/shard_map/ppermute | solution.py:204
  13.2 21.4 %collective-permute-start.17 = (bf16[64,2048]{1,0:T(8,128)(2,1)S(1)}, bf16[64,2048]{1,0:T(8,128)(2,1)S(1)}, u32[]{:S(2)}, u32[]{:S(2)}) collective-permute-start(bf16[64,2048]{1,0:T(8,128)(2,1)S(1)} %convert_element_type.169.refs_1_), channel_id=1, source_target_pairs={{0,3},{1,2},{2,1},{3,0},{4,7},{5,6},{6,5},{7,4},{8,11},{9,10},{10,... | collective-permute-start | bytes 786440 | tf_op jit(solution)/shard_map/ppermute | solution.py:207
  16.8 34.7 %collective-permute-start.18 = (bf16[64,2048]{1,0:T(8,128)(2,1)S(1)}, bf16[64,2048]{1,0:T(8,128)(2,1)S(1)}, u32[]{:S(2)}, u32[]{:S(2)}) collective-permute-start(bf16[64,2048]{1,0:T(8,128)(2,1)S(1)} %convert_element_type.169.refs_1_), channel_id=1, source_target_pairs={{0,2},{1,3},{2,0},{3,1},{4,6},{5,7},{6,4},{7,5},{8,10},{9,11},{10,... | collective-permute-start | bytes 786440 | tf_op jit(solution)/shard_map/ppermute | solution.py:207
  27.9 25.9 %collective-permute-start.7 = (bf16[64,2048]{1,0:T(8,128)(2,1)S(1)}, bf16[64,2048]{1,0:T(8,128)(2,1)S(1)}, u32[]{:S(2)}, u32[]{:S(2)}) collective-permute-start(bf16[64,2048]{1,0:T(8,128)(2,1)S(1)} %get-tuple-element.21), channel_id=1, source_target_pairs={{0,1},{1,0},{2,3},{3,2},{4,5},{5,4},{6,7},{7,6},{8,9},{9,8},{10,11... | collective-permute-start | bytes 786440 | tf_op jit(solution)/shard_map/ppermute | solution.py:207
  28.8 25.1 %collective-permute-start.8 = (bf16[64,2048]{1,0:T(8,128)(2,1)S(1)}, bf16[64,2048]{1,0:T(8,128)(2,1)S(1)}, u32[]{:S(2)}, u32[]{:S(2)}) collective-permute-start(bf16[64,2048]{1,0:T(8,128)(2,1)S(1)} %get-tuple-element.22), channel_id=1, source_target_pairs={{0,3},{1,2},{2,1},{3,0},{4,7},{5,6},{6,5},{7,4},{8,11},{9,10},{10,... | collective-permute-start | bytes 786440 | tf_op jit(solution)/shard_map/ppermute | solution.py:207
  32.4 29.4 %collective-permute-start.9 = (bf16[64,2048]{1,0:T(8,128)(2,1)S(1)}, bf16[64,2048]{1,0:T(8,128)(2,1)S(1)}, u32[]{:S(2)}, u32[]{:S(2)}) collective-permute-start(bf16[64,2048]{1,0:T(8,128)(2,1)S(1)} %get-tuple-element.23), channel_id=1, source_target_pairs={{0,2},{1,3},{2,0},{3,1},{4,6},{5,7},{6,4},{7,5},{8,10},{9,11},{10,... | collective-permute-start | bytes 786440 | tf_op jit(solution)/shard_map/ppermute | solution.py:207
  53.8 12.4 %collective-permute-start.20 = (bf16[4,64,1024]{2,1,0:T(8,128)(2,1)S(1)}, bf16[4,64,1024]{2,1,0:T(8,128)(2,1)S(1)}, u32[]{:S(2)}, u32[]{:S(2)}) collective-permute-start(bf16[4,64,1024]{2,1,0:T(8,128)(2,1)S(1)} %get-tuple-element.25), channel_id=1, source_target_pairs={{0,4},{4,0},{8,12},{12,8},{16,20},{20,16},{24,28},{28,24},{1,5},{5... | collective-permute-start | bytes 1572872 | tf_op jit(solution)/shard_map/ppermute | solution.py:204
  61.9 12.4 %collective-permute-start.33 = (bf16[64,2048]{1,0:T(8,128)(2,1)S(1)}, bf16[64,2048]{1,0:T(8,128)(2,1)S(1)}, u32[]{:S(2)}, u32[]{:S(2)}) collective-permute-start(bf16[64,2048]{1,0:T(8,128)(2,1)S(1)} %get-tuple-element.37.refs_1_), channel_id=1, source_target_pairs={{0,1},{1,0},{2,3},{3,2},{4,5},{5,4},{6,7},{7,6},{8,9},{9,8},{10,11... | collective-permute-start | bytes 786440 | tf_op jit(solution)/shard_map/ppermute | solution.py:207
  62.0 16.0 %collective-permute-start.31 = (bf16[64,2048]{1,0:T(8,128)(2,1)S(1)}, bf16[64,2048]{1,0:T(8,128)(2,1)S(1)}, u32[]{:S(2)}, u32[]{:S(2)}) collective-permute-start(bf16[64,2048]{1,0:T(8,128)(2,1)S(1)} %get-tuple-element.37.refs_1_), channel_id=1, source_target_pairs={{0,3},{1,2},{2,1},{3,0},{4,7},{5,6},{6,5},{7,4},{8,11},{9,10},{10,... | collective-permute-start | bytes 786440 | tf_op jit(solution)/shard_map/ppermute | solution.py:207
  64.5 22.9 %collective-permute-start.32 = (bf16[64,2048]{1,0:T(8,128)(2,1)S(1)}, bf16[64,2048]{1,0:T(8,128)(2,1)S(1)}, u32[]{:S(2)}, u32[]{:S(2)}) collective-permute-start(bf16[64,2048]{1,0:T(8,128)(2,1)S(1)} %get-tuple-element.37.refs_1_), channel_id=1, source_target_pairs={{0,2},{1,3},{2,0},{3,1},{4,6},{5,7},{6,4},{7,5},{8,10},{9,11},{10,... | collective-permute-start | bytes 786440 | tf_op jit(solution)/shard_map/ppermute | solution.py:207
  66.2 25.1 %collective-permute-start.21 = (bf16[64,1024]{1,0:T(8,128)(2,1)S(1)}, bf16[64,1024]{1,0:T(8,128)(2,1)S(1)}, u32[]{:S(2)}, u32[]{:S(2)}) collective-permute-start(bf16[64,1024]{1,0:T(8,128)(2,1)S(1)} %get-tuple-element.45), channel_id=1, source_target_pairs={{0,8},{4,12},{8,0},{12,4},{16,24},{20,28},{24,16},{28,20},{1,9},{5... | collective-permute-start | bytes 393224 | tf_op jit(solution)/shard_map/ppermute | solution.py:204
  67.5 25.5 %collective-permute-start.22 = (bf16[64,1024]{1,0:T(8,128)(2,1)S(1)}, bf16[64,1024]{1,0:T(8,128)(2,1)S(1)}, u32[]{:S(2)}, u32[]{:S(2)}) collective-permute-start(bf16[64,1024]{1,0:T(8,128)(2,1)S(1)} %get-tuple-element.47), channel_id=1, source_target_pairs={{0,16},{4,20},{8,24},{12,28},{16,0},{20,4},{24,8},{28,12},{1,17},{... | collective-permute-start | bytes 393224 | tf_op jit(solution)/shard_map/ppermute | solution.py:204
  74.3 18.7 %collective-permute-start.23 = (bf16[64,1024]{1,0:T(8,128)(2,1)S(1)}, bf16[64,1024]{1,0:T(8,128)(2,1)S(1)}, u32[]{:S(2)}, u32[]{:S(2)}) collective-permute-start(bf16[64,1024]{1,0:T(8,128)(2,1)S(1)} %get-tuple-element.46), channel_id=1, source_target_pairs={{0,24},{4,28},{8,16},{12,20},{16,8},{20,12},{24,0},{28,4},{1,25},{... | collective-permute-start | bytes 393224 | tf_op jit(solution)/shard_map/ppermute | solution.py:204
  78.0 16.1 %collective-permute-start.11 = (f32[64,64]{1,0:T(8,128)S(1)}, f32[64,64]{1,0:T(8,128)S(1)}, u32[]{:S(2)}, u32[]{:S(2)}) collective-permute-start(f32[64,64]{1,0:T(8,128)S(1)} %add.234), channel_id=1, source_target_pairs={{0,8},{4,12},{8,0},{12,4},{16,24},{20,28},{24,16},{28,20},{1,9},{5... | collective-permute-start | bytes 49160 | tf_op jit(solution)/shard_map/ppermute | solution.py:204
  87.4 6.7 %collective-permute-start.12 = (f32[64,64]{1,0:T(8,128)S(1)}, f32[64,64]{1,0:T(8,128)S(1)}, u32[]{:S(2)}, u32[]{:S(2)}) collective-permute-start(f32[64,64]{1,0:T(8,128)S(1)} %add.234), channel_id=1, source_target_pairs={{0,16},{4,20},{8,24},{12,28},{16,0},{20,4},{24,8},{28,12},{1,17},{... | collective-permute-start | bytes 49160 | tf_op jit(solution)/shard_map/ppermute | solution.py:204
  93.0 19.2 %collective-permute-start.34 = (bf16[4,64,1024]{2,1,0:T(8,128)(2,1)S(1)}, bf16[4,64,1024]{2,1,0:T(8,128)(2,1)S(1)}, u32[]{:S(2)}, u32[]{:S(2)}) collective-permute-start(bf16[4,64,1024]{2,1,0:T(8,128)(2,1)S(1)} %get-tuple-element.27), channel_id=1, source_target_pairs={{0,4},{4,0},{8,12},{12,8},{16,20},{20,16},{24,28},{28,24},{1,5},{5... | collective-permute-start | bytes 1572872 | tf_op jit(solution)/shard_map/ppermute | solution.py:204
  93.5 7.1 %collective-permute-start.24 = (f32[64,64]{1,0:T(8,128)S(1)}, f32[64,64]{1,0:T(8,128)S(1)}, u32[]{:S(2)}, u32[]{:S(2)}) collective-permute-start(f32[64,64]{1,0:T(8,128)S(1)} %fusion.44), channel_id=1, source_target_pairs={{0,4},{4,0},{8,12},{12,8},{16,20},{20,16},{24,28},{28,24},{1,5},{5... | collective-permute-start | bytes 49160 | tf_op jit(solution)/shard_map/ppermute | solution.py:204
  96.3 6.7 %collective-permute-start.15 = (f32[64,64]{1,0:T(8,128)S(1)}, f32[64,64]{1,0:T(8,128)S(1)}, u32[]{:S(2)}, u32[]{:S(2)}) collective-permute-start(f32[64,64]{1,0:T(8,128)S(1)} %add_add_fusion.10), channel_id=1, source_target_pairs={{0,2},{1,3},{2,0},{3,1},{4,6},{5,7},{6,4},{7,5},{8,10},{9,11},{10,... | collective-permute-start | bytes 49160 | tf_op jit(solution)/shard_map/ppermute | solution.py:207
  107.8 7.8 %collective-permute-start.28 = (f32[64,64]{1,0:T(8,128)S(1)}, f32[64,64]{1,0:T(8,128)S(1)}, u32[]{:S(2)}, u32[]{:S(2)}) collective-permute-start(f32[64,64]{1,0:T(8,128)S(1)} %add_add_fusion.8), channel_id=1, source_target_pairs={{0,1},{1,0},{2,3},{3,2},{4,5},{5,4},{6,7},{7,6},{8,9},{9,8},{10,11... | collective-permute-start | bytes 49160 | tf_op jit(solution)/shard_map/ppermute | solution.py:207
  108.0 9.3 %collective-permute-start.29 = (f32[64,64]{1,0:T(8,128)S(1)}, f32[64,64]{1,0:T(8,128)S(1)}, u32[]{:S(2)}, u32[]{:S(2)}) collective-permute-start(f32[64,64]{1,0:T(8,128)S(1)} %add_add_fusion.8), channel_id=1, source_target_pairs={{0,2},{1,3},{2,0},{3,1},{4,6},{5,7},{6,4},{7,5},{8,10},{9,11},{10,... | collective-permute-start | bytes 49160 | tf_op jit(solution)/shard_map/ppermute | solution.py:207
  110.9 6.4 %collective-permute-start.30 = (f32[64,64]{1,0:T(8,128)S(1)}, f32[64,64]{1,0:T(8,128)S(1)}, u32[]{:S(2)}, u32[]{:S(2)}) collective-permute-start(f32[64,64]{1,0:T(8,128)S(1)} %add_add_fusion.8), channel_id=1, source_target_pairs={{0,3},{1,2},{2,1},{3,0},{4,7},{5,6},{6,5},{7,4},{8,11},{9,10},{10,... | collective-permute-start | bytes 49160 | tf_op jit(solution)/shard_map/ppermute | solution.py:207
  113.8 11.1 %collective-permute-start.35 = (bf16[64,1024]{1,0:T(8,128)(2,1)}, bf16[64,1024]{1,0:T(8,128)(2,1)}, u32[]{:S(2)}, u32[]{:S(2)}) collective-permute-start(bf16[64,1024]{1,0:T(8,128)(2,1)} %get-tuple-element.42), channel_id=1, source_target_pairs={{0,8},{4,12},{8,0},{12,4},{16,24},{20,28},{24,16},{28,20},{1,9},{5... | collective-permute-start | bytes 393224 | tf_op jit(solution)/shard_map/ppermute | solution.py:204
  114.1 10.8 %collective-permute-start.36 = (bf16[64,1024]{1,0:T(8,128)(2,1)S(1)}, bf16[64,1024]{1,0:T(8,128)(2,1)}, u32[]{:S(2)}, u32[]{:S(2)}) collective-permute-start(bf16[64,1024]{1,0:T(8,128)(2,1)S(1)} %get-tuple-element.44), channel_id=1, source_target_pairs={{0,16},{4,20},{8,24},{12,28},{16,0},{20,4},{24,8},{28,12},{1,17},{... | collective-permute-start | bytes 393224 | tf_op jit(solution)/shard_map/ppermute | solution.py:204
  115.6 9.2 %collective-permute-start.37 = (bf16[64,1024]{1,0:T(8,128)(2,1)S(1)}, bf16[64,1024]{1,0:T(8,128)(2,1)}, u32[]{:S(2)}, u32[]{:S(2)}) collective-permute-start(bf16[64,1024]{1,0:T(8,128)(2,1)S(1)} %get-tuple-element.43), channel_id=1, source_target_pairs={{0,24},{4,28},{8,16},{12,20},{16,8},{20,12},{24,0},{28,4},{1,25},{... | collective-permute-start | bytes 393224 | tf_op jit(solution)/shard_map/ppermute | solution.py:204
  126.5 10.4 %collective-permute-start.39 = (bf16[64,1024]{1,0:T(8,128)(2,1)S(1)}, bf16[64,1024]{1,0:T(8,128)(2,1)S(1)}, u32[]{:S(2)}, u32[]{:S(2)}) collective-permute-start(bf16[64,1024]{1,0:T(8,128)(2,1)S(1)} %get-tuple-element.50.refs_0_), channel_id=1, source_target_pairs={{0,8},{4,12},{8,0},{12,4},{16,24},{20,28},{24,16},{28,20},{1,9},{5... | collective-permute-start | bytes 393224 | tf_op jit(solution)/shard_map/ppermute | solution.py:204
  126.9 10.5 %collective-permute-start.41 = (bf16[64,1024]{1,0:T(8,128)(2,1)S(1)}, bf16[64,1024]{1,0:T(8,128)(2,1)S(1)}, u32[]{:S(2)}, u32[]{:S(2)}) collective-permute-start(bf16[64,1024]{1,0:T(8,128)(2,1)S(1)} %get-tuple-element.50.refs_0_), channel_id=1, source_target_pairs={{0,16},{4,20},{8,24},{12,28},{16,0},{20,4},{24,8},{28,12},{1,17},{... | collective-permute-start | bytes 393224 | tf_op jit(solution)/shard_map/ppermute | solution.py:204
  128.4 9.1 %collective-permute-start.43 = (bf16[64,1024]{1,0:T(8,128)(2,1)S(1)}, bf16[64,1024]{1,0:T(8,128)(2,1)S(1)}, u32[]{:S(2)}, u32[]{:S(2)}) collective-permute-start(bf16[64,1024]{1,0:T(8,128)(2,1)S(1)} %get-tuple-element.50.refs_0_), channel_id=1, source_target_pairs={{0,24},{4,28},{8,16},{12,20},{16,8},{20,12},{24,0},{28,4},{1,25},{... | collective-permute-start | bytes 393224 | tf_op jit(solution)/shard_map/ppermute | solution.py:204
  136.9 6.7 %collective-permute-start.40 = (bf16[64,1024]{1,0:T(8,128)(2,1)S(1)}, bf16[64,1024]{1,0:T(8,128)(2,1)S(1)}, u32[]{:S(2)}, u32[]{:S(2)}) collective-permute-start(bf16[64,1024]{1,0:T(8,128)(2,1)S(1)} %collective-permute-done.39.refs_2_), channel_id=1, source_target_pairs={{0,4},{4,0},{8,12},{12,8},{16,20},{20,16},{24,28},{28,24},{1,5},{5... | collective-permute-start | bytes 393224 | tf_op jit(solution)/shard_map/ppermute | solution.py:204
  137.4 7.5 %collective-permute-start.42 = (bf16[64,1024]{1,0:T(8,128)(2,1)S(1)}, bf16[64,1024]{1,0:T(8,128)(2,1)S(1)}, u32[]{:S(2)}, u32[]{:S(2)}) collective-permute-start(bf16[64,1024]{1,0:T(8,128)(2,1)S(1)} %collective-permute-done.41.refs_4_), channel_id=1, source_target_pairs={{0,4},{4,0},{8,12},{12,8},{16,20},{20,16},{24,28},{28,24},{1,5},{5... | collective-permute-start | bytes 393224 | tf_op jit(solution)/shard_map/ppermute | solution.py:204
  137.5 7.4 %collective-permute-start.44 = (bf16[64,1024]{1,0:T(8,128)(2,1)S(1)}, bf16[64,1024]{1,0:T(8,128)(2,1)S(1)}, u32[]{:S(2)}, u32[]{:S(2)}) collective-permute-start(bf16[64,1024]{1,0:T(8,128)(2,1)S(1)} %collective-permute-done.43.refs_6_), channel_id=1, source_target_pairs={{0,4},{4,0},{8,12},{12,8},{16,20},{20,16},{24,28},{28,24},{1,5},{5... | collective-permute-start | bytes 393224 | tf_op jit(solution)/shard_map/ppermute | solution.py:204
  140.5 21.7 %collective-permute-start.52 = (f32[64,64]{1,0:T(8,128)S(1)}, f32[64,64]{1,0:T(8,128)S(1)}, u32[]{:S(2)}, u32[]{:S(2)}) collective-permute-start(f32[64,64]{1,0:T(8,128)S(1)} %add_add_fusion.6), channel_id=1, source_target_pairs={{0,1},{1,0},{2,3},{3,2},{4,5},{5,4},{6,7},{7,6},{8,9},{9,8},{10,11... | collective-permute-start | bytes 49160 | tf_op jit(solution)/shard_map/ppermute | solution.py:207
  140.6 22.6 %collective-permute-start.53 = (f32[64,64]{1,0:T(8,128)S(1)}, f32[64,64]{1,0:T(8,128)S(1)}, u32[]{:S(2)}, u32[]{:S(2)}) collective-permute-start(f32[64,64]{1,0:T(8,128)S(1)} %add_add_fusion.6), channel_id=1, source_target_pairs={{0,2},{1,3},{2,0},{3,1},{4,6},{5,7},{6,4},{7,5},{8,10},{9,11},{10,... | collective-permute-start | bytes 49160 | tf_op jit(solution)/shard_map/ppermute | solution.py:207
  143.6 19.5 %collective-permute-start.54 = (f32[64,64]{1,0:T(8,128)S(1)}, f32[64,64]{1,0:T(8,128)S(1)}, u32[]{:S(2)}, u32[]{:S(2)}) collective-permute-start(f32[64,64]{1,0:T(8,128)S(1)} %add_add_fusion.6), channel_id=1, source_target_pairs={{0,3},{1,2},{2,1},{3,0},{4,7},{5,6},{6,5},{7,4},{8,11},{9,10},{10,... | collective-permute-start | bytes 49160 | tf_op jit(solution)/shard_map/ppermute | solution.py:207
  159.6 12.6 %collective-permute-start.45 = (bf16[64,2048]{1,0:T(8,128)(2,1)S(1)}, bf16[64,2048]{1,0:T(8,128)(2,1)S(1)}, u32[]{:S(2)}, u32[]{:S(2)}) collective-permute-start(bf16[64,2048]{1,0:T(8,128)(2,1)S(1)} %get-tuple-element.30), channel_id=1, source_target_pairs={{0,1},{1,0},{2,3},{3,2},{4,5},{5,4},{6,7},{7,6},{8,9},{9,8},{10,11... | collective-permute-start | bytes 786440 | tf_op jit(solution)/shard_map/ppermute | solution.py:207
  159.6 14.4 %collective-permute-start.46 = (bf16[64,2048]{1,0:T(8,128)(2,1)S(1)}, bf16[64,2048]{1,0:T(8,128)(2,1)S(1)}, u32[]{:S(2)}, u32[]{:S(2)}) collective-permute-start(bf16[64,2048]{1,0:T(8,128)(2,1)S(1)} %get-tuple-element.31), channel_id=1, source_target_pairs={{0,3},{1,2},{2,1},{3,0},{4,7},{5,6},{6,5},{7,4},{8,11},{9,10},{10,... | collective-permute-start | bytes 786440 | tf_op jit(solution)/shard_map/ppermute | solution.py:207
  162.2 20.7 %collective-permute-start.47 = (bf16[64,2048]{1,0:T(8,128)(2,1)S(1)}, bf16[64,2048]{1,0:T(8,128)(2,1)S(1)}, u32[]{:S(2)}, u32[]{:S(2)}) collective-permute-start(bf16[64,2048]{1,0:T(8,128)(2,1)S(1)} %get-tuple-element.32), channel_id=1, source_target_pairs={{0,2},{1,3},{2,0},{3,1},{4,6},{5,7},{6,4},{7,5},{8,10},{9,11},{10,... | collective-permute-start | bytes 786440 | tf_op jit(solution)/shard_map/ppermute | solution.py:207
  183.1 11.6 %collective-permute-start.64 = (bf16[64,2048]{1,0:T(8,128)(2,1)S(1)}, bf16[64,2048]{1,0:T(8,128)(2,1)S(1)}, u32[]{:S(2)}, u32[]{:S(2)}) collective-permute-start(bf16[64,2048]{1,0:T(8,128)(2,1)S(1)} %get-tuple-element.35.refs_1_), channel_id=1, source_target_pairs={{0,1},{1,0},{2,3},{3,2},{4,5},{5,4},{6,7},{7,6},{8,9},{9,8},{10,11... | collective-permute-start | bytes 786440 | tf_op jit(solution)/shard_map/ppermute | solution.py:207
  183.1 27.3 %collective-permute-start.62 = (bf16[64,2048]{1,0:T(8,128)(2,1)S(1)}, bf16[64,2048]{1,0:T(8,128)(2,1)S(1)}, u32[]{:S(2)}, u32[]{:S(2)}) collective-permute-start(bf16[64,2048]{1,0:T(8,128)(2,1)S(1)} %get-tuple-element.35.refs_1_), channel_id=1, source_target_pairs={{0,3},{1,2},{2,1},{3,0},{4,7},{5,6},{6,5},{7,4},{8,11},{9,10},{10,... | collective-permute-start | bytes 786440 | tf_op jit(solution)/shard_map/ppermute | solution.py:207
  185.7 24.8 %collective-permute-start.63 = (bf16[64,2048]{1,0:T(8,128)(2,1)S(1)}, bf16[64,2048]{1,0:T(8,128)(2,1)S(1)}, u32[]{:S(2)}, u32[]{:S(2)}) collective-permute-start(bf16[64,2048]{1,0:T(8,128)(2,1)S(1)} %get-tuple-element.35.refs_1_), channel_id=1, source_target_pairs={{0,2},{1,3},{2,0},{3,1},{4,6},{5,7},{6,4},{7,5},{8,10},{9,11},{10,... | collective-permute-start | bytes 786440 | tf_op jit(solution)/shard_map/ppermute | solution.py:207
  188.5 28.6 %collective-permute-start.56 = (f32[64,64]{1,0:T(8,128)S(1)}, f32[64,64]{1,0:T(8,128)S(1)}, u32[]{:S(2)}, u32[]{:S(2)}) collective-permute-start(f32[64,64]{1,0:T(8,128)S(1)} %add.276), channel_id=1, source_target_pairs={{0,8},{4,12},{8,0},{12,4},{16,24},{20,28},{24,16},{28,20},{1,9},{5... | collective-permute-start | bytes 49160 | tf_op jit(solution)/shard_map/ppermute | solution.py:204
  189.0 28.0 %collective-permute-start.57 = (f32[64,64]{1,0:T(8,128)S(1)}, f32[64,64]{1,0:T(8,128)S(1)}, u32[]{:S(2)}, u32[]{:S(2)}) collective-permute-start(f32[64,64]{1,0:T(8,128)S(1)} %add.276), channel_id=1, source_target_pairs={{0,16},{4,20},{8,24},{12,28},{16,0},{20,4},{24,8},{28,12},{1,17},{... | collective-permute-start | bytes 49160 | tf_op jit(solution)/shard_map/ppermute | solution.py:204
  194.6 22.4 %collective-permute-start.58 = (f32[64,64]{1,0:T(8,128)S(1)}, f32[64,64]{1,0:T(8,128)S(1)}, u32[]{:S(2)}, u32[]{:S(2)}) collective-permute-start(f32[64,64]{1,0:T(8,128)S(1)} %add.276), channel_id=1, source_target_pairs={{0,24},{4,28},{8,16},{12,20},{16,8},{20,12},{24,0},{28,4},{1,25},{... | collective-permute-start | bytes 49160 | tf_op jit(solution)/shard_map/ppermute | solution.py:204
  217.0 14.4 %collective-permute-start.65 = (bf16[4,64,1024]{2,1,0:T(8,128)(2,1)S(1)}, bf16[4,64,1024]{2,1,0:T(8,128)(2,1)}, u32[]{:S(2)}, u32[]{:S(2)}) collective-permute-start(bf16[4,64,1024]{2,1,0:T(8,128)(2,1)S(1)} %get-tuple-element.34), channel_id=1, source_target_pairs={{0,4},{4,0},{8,12},{12,8},{16,20},{20,16},{24,28},{28,24},{1,5},{5... | collective-permute-start | bytes 1572872 | tf_op jit(solution)/shard_map/ppermute | solution.py:204
  232.9 7.8 %collective-permute-start.67 = (bf16[64,1024]{1,0:T(8,128)(2,1)S(1)}, bf16[64,1024]{1,0:T(8,128)(2,1)S(1)}, u32[]{:S(2)}, u32[]{:S(2)}) collective-permute-start(bf16[64,1024]{1,0:T(8,128)(2,1)S(1)} %get-tuple-element.41), channel_id=1, source_target_pairs={{0,16},{4,20},{8,24},{12,28},{16,0},{20,4},{24,8},{28,12},{1,17},{... | collective-permute-start | bytes 393224 | tf_op jit(solution)/shard_map/ppermute | solution.py:204
  (48 other events, 363.0 us)
